TPU v7x, 256 devices: a whole 4x4x8 slice. The times are simulated.
256 devices in a mesh: dp: 64 (over y, z_lo, x, core), mp: 4 (over z_hi).
Axes of the slice: x: 4, y: 4, z: 8 (z_hi: 4, z_lo: 2; z = z_hi * 2 + z_lo), core: 2. Of those that a mesh axis runs over, the one named last changes fastest.
Arguments:
- clips: bfloat16 [8192, 768], P('dp', 'mp')
- captions: bfloat16 [8192, 768], P('dp', 'mp')
- video_id: int32 [8192], replicated, may hold values from 0 to 511, never falling along the last dimension, each value on 1 to 128 neighbouring positions
- logit_scale: float32 [], replicated, may hold values from 110 to 160
Outputs:
- d_clips: float32 [8192, 768], P(('dp', 'mp'))
- d_captions: float32 [8192, 768], P(('dp', 'mp'))
Inputs may be any that keep to these rules, and one draw needn't show every extreme that they name: `video_id`: video ids never fall along the rows; each video covers 1 to 128 consecutive rows.
All inputs are finite; a program needn't handle non-finite values.
Results may differ from a plain program's by a relative error of at most 0.0095.
Values may be sent and summed in bfloat16 or wider, within the bound.
A program may use at most 64 MiB of HBM per device.

v0:
```python
import jax
import jax.numpy as jnp
from jax import lax
from jax.sharding import PartitionSpec as P

epsilon = 1e-06
negative_fill = -1e30


def extended(value, sides, width):
    for axis, dim in sides:
        size, length = (lax.axis_size(axis), value.shape[dim])
        up = [(i, (i + 1) % size) for i in range(size - 1)]
        down = [(j, i) for i, j in up]
        last = lax.slice_in_dim(value, length - width, length, axis=dim)
        leading = lax.slice_in_dim(value, 0, width, axis=dim)
        before = lax.ppermute(last, axis, up)
        after = lax.ppermute(leading, axis, down)
        value = jnp.concatenate([before, value, after], axis=dim)
    return value


def shifted(block, axis, distance):
    devices = range(lax.axis_size(axis))
    route = [((i - distance) % len(devices), i) for i in devices]
    return lax.ppermute(block, axis, route)


def combined_all(value, axis, combine):
    everything = jax.tree.map(lambda part: lax.all_gather(part, axis), value)
    leading = jax.tree.map(lambda part: part[0], everything)

    def lap(k, so_far):
        return combine(so_far, jax.tree.map(lambda part: part[k], everything))

    return lax.fori_loop(1, lax.axis_size(axis), lap, leading)


def unit_rows(values):
    widened = values.astype(jnp.float32)
    length = jnp.sqrt(jnp.sum(widened * widened, axis=-1) + epsilon)
    return (widened / length[:, None], length)


def tile_scores(caption_panel, clip_unit, logit_scale):
    return logit_scale * lax.dot_general(
        caption_panel, clip_unit, (((1,), (1,)), ((), ())), preferred_element_type=jnp.float32
    )


def forward_update(running, scores, allowed):
    row_max, row_sum, col_max, col_sum = running
    masked = jnp.where(allowed, scores, negative_fill)
    new_row = jnp.maximum(row_max, jnp.max(masked, axis=0))
    new_col = jnp.maximum(col_max, jnp.max(masked, axis=1))
    row_terms = jnp.exp(scores - new_row[None, :])
    col_terms = jnp.exp(scores - new_col[:, None])
    row_terms = jnp.where(allowed, row_terms, 0.0)
    col_terms = jnp.where(allowed, col_terms, 0.0)
    row_sum = row_sum * jnp.exp(row_max - new_row) + jnp.sum(row_terms, axis=0)
    col_sum = col_sum * jnp.exp(col_max - new_col) + jnp.sum(col_terms, axis=1)
    return (new_row, row_sum, new_col, col_sum)


def backward_update(
    accumulated, scores, allowed, same_video, caption_panel, clip_unit, row_lse, col_lse
):
    clip_acc, pool_acc, cap_acc = accumulated
    weights = 0.5 * (jnp.exp(scores - row_lse[None, :]) + jnp.exp(scores - col_lse[:, None]))
    weights = jnp.where(allowed, weights, 0.0)
    weights = weights.astype(jnp.bfloat16)
    clip_acc = clip_acc + lax.dot_general(
        weights, caption_panel, (((0,), (0,)), ((), ())), preferred_element_type=jnp.float32
    )
    cap_acc = cap_acc + jnp.dot(weights, clip_unit, preferred_element_type=jnp.float32)
    pool_acc = pool_acc + lax.dot_general(
        same_video.astype(jnp.bfloat16),
        caption_panel,
        (((0,), (0,)), ((), ())),
        preferred_element_type=jnp.float32,
    )
    return (clip_acc, pool_acc, cap_acc)


def join_stats(left_pair, right_pair):
    top_value = jnp.maximum(left_pair[0], right_pair[0])
    return (
        top_value,
        left_pair[1] * jnp.exp(left_pair[0] - top_value)
        + right_pair[1] * jnp.exp(right_pair[0] - top_value),
    )


def body(clips, captions, video_id, logit_scale):
    dp_count = lax.axis_size("dp")
    mp_count = lax.axis_size("mp")
    row_count = clips.shape[0]
    sub_rows = row_count // mp_count
    feature_width = clips.shape[1] * mp_count
    dp_index = lax.axis_index("dp")
    mp_index = lax.axis_index("mp")
    full_clips = lax.all_gather(clips, "mp", axis=1, tiled=True)
    home_captions = lax.all_to_all(captions, "mp", split_axis=0, concat_axis=1, tiled=True)
    clip_float, clip_length = unit_rows(full_clips)
    clip_unit = clip_float.astype(jnp.bfloat16)
    cap_float, cap_length = unit_rows(home_captions)
    cap_unit = cap_float.astype(jnp.bfloat16)
    all_rows = video_id.shape[0]
    first_clip = dp_index * row_count
    clip_positions = first_clip + jnp.arange(row_count, dtype=jnp.int32)
    clip_videos = lax.dynamic_slice_in_dim(video_id, first_clip, row_count, 0)
    same_block = (clip_videos[:, None] == clip_videos[None, :]).astype(jnp.bfloat16)
    local_pool = jnp.dot(same_block, clip_unit, preferred_element_type=jnp.float32)
    edge_sums = jnp.stack([local_pool[0], local_pool[row_count - 1]])
    beside = extended(edge_sums, (("dp", 0),), 1)
    left_video = lax.dynamic_index_in_dim(
        video_id, jnp.maximum(first_clip - 1, 0), 0, keepdims=False
    )
    right_video = lax.dynamic_index_in_dim(
        video_id, jnp.minimum(first_clip + row_count, all_rows - 1), 0, keepdims=False
    )
    from_left = ((clip_videos == left_video) & (dp_index > 0)).astype(jnp.float32)
    from_right = ((clip_videos == right_video) & (dp_index < dp_count - 1)).astype(jnp.float32)
    pooled = (
        local_pool
        + from_left[:, None] * beside[0][None, :]
        + from_right[:, None] * beside[3][None, :]
    )
    pool_length = jnp.sqrt(jnp.sum(pooled * pooled, axis=-1) + epsilon)
    pool_unit = pooled / pool_length[:, None]

    def tile_masks(first_row):
        panel_videos = lax.dynamic_slice_in_dim(video_id, first_row, sub_rows, 0)
        panel_positions = first_row + jnp.arange(sub_rows, dtype=jnp.int32)
        same_video = panel_videos[:, None] == clip_videos[None, :]
        allowed = jnp.logical_not(same_video) | (
            panel_positions[:, None] == clip_positions[None, :]
        )
        return (allowed, same_video)

    def source_first(turn_index):
        source_index = (dp_index - turn_index) % dp_count
        return (source_index, source_index * row_count + mp_index * sub_rows)

    def forward_step(turn_index, caption_panel, running):
        source_index, first_row = source_first(turn_index)
        scores = tile_scores(caption_panel, clip_unit, logit_scale)
        allowed, same_video = tile_masks(first_row)
        return forward_update(running, scores, allowed)

    def send_panel(caption_panel):
        return shifted(caption_panel, "dp", 1)

    def send_stats(stat_pair):
        return shifted(stat_pair, "dp", 1)

    panel_store = jnp.zeros((1,), jnp.bfloat16)
    running = (
        jnp.full((row_count,), negative_fill, jnp.float32),
        jnp.zeros((row_count,), jnp.float32),
        jnp.full((sub_rows,), negative_fill, jnp.float32),
        jnp.zeros((sub_rows,), jnp.float32),
    )

    def forward_turn(turn_index, state_tuple):
        caption_panel, current, stored = state_tuple
        current = forward_step(turn_index, caption_panel, current)
        col_pair = send_stats((current[2], current[3]))
        return (
            send_panel(caption_panel),
            (current[0], current[1], col_pair[0], col_pair[1]),
            stored,
        )

    caption_panel, running, panel_store = lax.fori_loop(
        0, dp_count - 1, forward_turn, (cap_unit, running, panel_store)
    )
    running = forward_step(dp_count - 1, caption_panel, running)
    col_max, col_sum = send_stats((running[2], running[3]))
    row_max, row_sum = combined_all((running[0], running[1]), "mp", join_stats)
    row_lse = row_max + jnp.log(row_sum)
    col_lse = col_max + jnp.log(col_sum)

    def backward_step(turn_index, caption_panel, col_lse_now, accumulated):
        source_index, first_row = source_first(turn_index)
        scores = tile_scores(caption_panel, clip_unit, logit_scale)
        allowed, same_video = tile_masks(first_row)
        return backward_update(
            accumulated, scores, allowed, same_video, caption_panel, clip_unit, row_lse, col_lse_now
        )

    def send_sums(sum_pair):
        return shifted(sum_pair, "dp", 1)

    def send_back(caption_panel):
        return shifted(caption_panel, "dp", 1)

    def backward_turn(turn_index, state_tuple):
        caption_panel, sum_pair, clip_acc, pool_acc = state_tuple
        current_panel = caption_panel
        clip_acc, pool_acc, cap_acc = backward_step(
            turn_index, current_panel, sum_pair[0], (clip_acc, pool_acc, sum_pair[1])
        )
        sum_pair = send_sums((sum_pair[0], cap_acc))
        caption_panel = send_back(caption_panel)
        return (caption_panel, sum_pair, clip_acc, pool_acc)

    zero_clips = jnp.zeros((row_count, feature_width), jnp.float32)
    start_state = (
        cap_unit,
        (col_lse, jnp.zeros((sub_rows, feature_width), jnp.float32)),
        zero_clips,
        zero_clips,
    )
    caption_panel, sum_pair, clip_acc, pool_acc = lax.fori_loop(
        0, dp_count - 1, backward_turn, start_state
    )
    current_panel = caption_panel
    clip_acc, pool_acc, cap_acc = backward_step(
        dp_count - 1, current_panel, sum_pair[0], (clip_acc, pool_acc, sum_pair[1])
    )
    sum_pair = send_sums((sum_pair[0], cap_acc))
    cap_acc = sum_pair[1]
    projected = pool_acc - pool_unit * jnp.sum(pool_unit * pool_acc, axis=-1, keepdims=True)
    partial_grad = logit_scale * clip_acc - 0.5 * logit_scale * projected / pool_length[:, None]
    own_first = mp_index * sub_rows
    own_rows = lax.dynamic_slice_in_dim(
        partial_grad, own_first, sub_rows, 0
    ) - 0.5 * logit_scale * cap_unit.astype(jnp.float32)
    partial_grad = lax.dynamic_update_slice_in_dim(partial_grad, own_rows, own_first, 0)
    clip_grad_unit = lax.psum_scatter(
        partial_grad.astype(jnp.bfloat16), "mp", scatter_dimension=0, tiled=True
    ).astype(jnp.float32)
    sub_float = lax.dynamic_slice_in_dim(clip_float, own_first, sub_rows, 0)
    sub_length = lax.dynamic_slice_in_dim(clip_length, own_first, sub_rows, 0)
    sub_clip_unit = lax.dynamic_slice_in_dim(clip_unit, own_first, sub_rows, 0).astype(jnp.float32)
    sub_pool_unit = lax.dynamic_slice_in_dim(pool_unit, own_first, sub_rows, 0)
    d_clips = (
        clip_grad_unit - sub_float * jnp.sum(sub_float * clip_grad_unit, axis=-1, keepdims=True)
    ) / sub_length[:, None]
    cap_grad_unit = (
        logit_scale * cap_acc
        - 0.5 * logit_scale * sub_clip_unit
        - 0.5 * logit_scale * sub_pool_unit
    )
    d_captions = (
        cap_grad_unit - cap_float * jnp.sum(cap_float * cap_grad_unit, axis=-1, keepdims=True)
    ) / cap_length[:, None]
    return (d_clips, d_captions)


def solution(mesh):
    in_specs = (P("dp", "mp"), P("dp", "mp"), P(), P())
    out_specs = (P(("dp", "mp"), None), P(("dp", "mp"), None))
    return jax.shard_map(body, mesh=mesh, in_specs=in_specs, out_specs=out_specs, check_vma=False)
```

profile of v0, /device:TPU:1, one launch (start us, length us, event | category | flops | bytes accessed | tf_op | source)
XLA Modules:
  0.0 1352.4 jit_solution(9119368713345172676)
XLA Ops:
  8.7 9.1 all-to-all-start
  17.8 13.7 %all_gather.15 = bf16[128,768]{0,1:T(8,128)(2,1)S(1)} all-gather(bf16[128,192]{0,1:T(8,128)(2,1)S(1)} %copy-done.1), channel_id=1, replica_groups=mesh['dp'=64,'mp'=4] {'mp'}, dimensions={1}, use_global_device_ids=true | all-gather | bytes 245760 | tf_op jit(solution)/shard_map/all_gather | solution.py:102
  34.9 6.9 collective-permute-start.8
  47.5 591.7 %while.66 = (s32[]{:T(128)}, bf16[32,768]{1,0:T(8,128)(2,1)S(1)}, f32[128]{0:T(128)S(1)}, f32[128]{0:T(128)S(1)}, f32[32]{0:T(128)S(1)}, /*index=5*/f32[32]{0:T(...) while((s32[]{:T(128)}, bf16[32,768]{1,0:T(8,128)(2,1)S(1)}, ...), condition=%wide.region_7.8_spmd.clone, body=%wide.region_2.7_spmd.clone.sunk | while | flops 6366068 | bytes 586739 | solution.py:175
  92.0 6.9 collective-permute-done.1
  129.9 6.9 collective-permute-done.1
  139.4 6.9 collective-permute-done.1
  177.3 6.9 collective-permute-done.1
  186.8 6.9 collective-permute-done.1
  224.7 6.9 collective-permute-done.1
  272.0 6.9 collective-permute-done.1
  309.9 6.9 collective-permute-done.1
  319.4 6.9 collective-permute-done.1
  357.3 6.9 collective-permute-done.1
  366.8 6.9 collective-permute-done.1
  404.7 6.9 collective-permute-done.1
  452.0 6.9 collective-permute-done.1
  489.9 6.9 collective-permute-done.1
  639.8 7.3 all-gather.3
  647.1 8.6 all-gather.2
  656.0 11.2 collective-permute-done.7
  667.2 646.4 %while.67 = (s32[]{:T(128)}, bf16[32,768]{1,0:T(8,128)(2,1)S(1)}, f32[32]{0:T(128)S(1)}, f32[32,768]{1,0:T(8,128)S(1)}, f32[128,768]{1,0:T(8,128)S(1)}, /*index=...) while((s32[]{:T(128)}, bf16[32,768]{1,0:T(8,128)(2,1)S(1)}, ...), condition=%wide.region_15.16_spmd.clone, body=%wide.region_14.15_spmd.clone.sunk | while | flops 25632948 | bytes 3027579 | solution.py:215
  1316.0 6.9 collective-permute-done.10
  1323.9 20.0 %reduce-scatter.2.cloned.1.call-done = bf16[32,768]{1,0:T(8,128)(2,1)} async-done(((bf16[128,768]{1,0:T(8,128)(2,1)}), bf16[32,768]{1,0:T(8,128)(2,1)}) %reduce-scatter.2.cloned.1.call-update) | async-done | bytes 49168 | tf_op jit(solution)/shard_map/reduce_scatter | solution.py:231
  (2138 shorter events, 1144.1 us)
Async XLA Ops:
  8.7 38.3 %all-to-all-start = ((bf16[4,32,192]{2,1,0:T(8,128)(2,1)}), bf16[4,32,192]{2,1,0:T(8,128)(2,1)S(1)}, u32[]{:S(2)}, u32[]{:S(2)}) async-start(bf16[4,32,192]{2,1,0:T(8,128)(2,1)} %bitcast.2), calls=%async_computation | async-start | bytes 131072 | tf_op jit(solution)/shard_map/all_to_all | solution.py:103
  17.8 1326.0 %reduce-scatter.2.cloned.1.call-start = ((), (), s32[]{:S(2)}) async-start(), calls=%async_computation.2 | async-start | bytes 245760 | tf_op jit(solution)/shard_map/reduce_scatter | solution.py:231
  34.9 11.0 collective-permute-start.8
  61.3 9.5 collective-permute-start
  70.8 9.5 collective-permute-start
  108.7 9.5 collective-permute-start
  118.2 9.5 collective-permute-start
  146.6 9.5 collective-permute-start
  156.1 9.5 collective-permute-start
  165.5 9.5 collective-permute-start
  194.0 9.5 collective-permute-start
  203.4 9.5 collective-permute-start
  241.3 9.5 collective-permute-start
  250.8 9.5 collective-permute-start
  288.7 9.5 collective-permute-start
  298.2 9.5 collective-permute-start
  326.6 9.5 collective-permute-start
  336.1 9.5 collective-permute-start
  345.5 9.5 collective-permute-start
  374.0 9.5 collective-permute-start
  383.4 9.5 collective-permute-start
  421.3 9.5 collective-permute-start
  639.5 27.7 %collective-permute-start.6 = (f32[32]{0:T(128)S(1)}, f32[32]{0:T(128)S(1)}, u32[]{:S(2)}, u32[]{:S(2)}) collective-permute-start(f32[32]{0:T(128)S(1)} %max.39), channel_id=1, source_target_pairs={{252,0},{0,4},{4,8},{8,12},{12,16},{16,20},{20,24},{24,28},{28,32}... | collective-permute-start | bytes 392 | tf_op jit(solution)/shard_map/ppermute | solution.py:26
  655.9 11.3 collective-permute-start.7
  (363 other events, 2890.4 us)
Sparse Core Ops, SparseCore 0:
  1316.0 27.7 reduce-scatter.1
where the time goes:
time: 1360 us; the launch traced here: 1350 us
  waiting for transfers between devices  951 us (70%)
  matrix products  164 us (12%)
  local copies, waits for them, and re-layouts  101 us (7%)
  starting transfers between devices  56.4 us (4%)
  blocking collectives  29.6 us (2%)
  other arithmetic  21.9 us (2%)
  between operations  15 us (1%)
  loops' own time  13.6 us (1%)
    ppermute x381, waiting for transfers between devices, shifted(): return lax.ppermute(block, axis, route)  930 us
    dot_general x128, matrix products, tile_scores(): lax.dot_general(caption_panel, clip_unit, (((1,), (1,)), ((), ())), prefe...  113 us
    dynamic_slice x127, local copies, waits for them, and re-layouts, tile_masks(): panel_videos = lax.dynamic_slice_in_dim(video_id, first_row, sub_rows, 0)  97 us
    ppermute x381, starting transfers between devices, shifted(): return lax.ppermute(block, axis, route)  38.5 us
  transfers between devices with their start and end apart: 385, of which 255 were waited for; matrix products, arithmetic and copies ran while one was open for 21% of the time, Pallas kernels for 0%

commit v1 on v0

v1 whole, which is shorter than its diff:
```python
import jax
import jax.numpy as jnp
from jax import lax
from jax.experimental import pallas as pl
from jax.experimental.pallas import tpu as pltpu
from jax.sharding import PartitionSpec as P

EPSILON = 1e-06
NEGATIVE_FILL = -1e30
F32 = jnp.float32
BF16 = jnp.bfloat16
MESH = pl.DeviceIdType.MESH


def chip(x, y, z, core):
    return ((y * 2 + lax.rem(z, 2)) * 8 + x * 2 + core, lax.div(z, 2))


def kernel(
    scale_ref, vid_ref, clips_ref, caps_ref,
    dclip_ref, dcap_ref,
    ca, ta, hclip, hcap, hlen,
    cl, ct, vi, vj,
    pu, plen, eo, ei,
    sc, same, wt, pj,
    rst, rsib, rcomb, rz, cst, cx, ccomb, cy,
    g, sb, hb, hown, rzs,
    g2, pc, qy, qx, r0, r1, r0b, r1b, fx, fy,
    a2a_s, a2a_r, z_s, z_r, s_s, s_r, p_s, p_r, e_s, e_r,
    t_s, t_r, u_s, u_r, w_s, w_r, v_s, v_r,
):
    dp = lax.axis_index("dp")
    zh = lax.axis_index("mp")
    core = lax.rem(dp, 2)
    x = lax.rem(lax.div(dp, 2), 4)
    zl = lax.rem(lax.div(dp, 8), 2)
    y = lax.div(dp, 16)
    z = zh * 2 + zl
    mine = zl * 8 + core * 4 + zh
    sibling = chip(x, y, z, 1 - core)
    at_z = lambda d: chip(x, y, lax.rem(z + d, 8), core)
    at_x = lambda d: chip(lax.rem(x + d, 4), y, z, core)
    at_y = lambda d: chip(x, lax.rem(y + d, 4), z, core)

    def copy(src, dst, send, recv, device):
        c = pltpu.make_async_remote_copy(
            src_ref=src, dst_ref=dst, send_sem=send, recv_sem=recv,
            device_id=device, device_id_type=MESH,
        )
        c.start()
        return c

    runs = [y * 8 + x, y * 8 + 4 + x]

    def owner(q):
        return chip(lax.rem(q, 4), lax.div(q, 8), z, core), lax.rem(lax.div(q, 4), 2)

    after = [owner(lax.rem(q + 1, 32)) for q in runs]
    before = [owner(lax.rem(q + 31, 32)) for q in runs]

    barrier = pltpu.get_barrier_semaphore()
    partners = [sibling] + [at_z(d) for d in range(1, 8)]
    partners += [at_x(d) for d in range(1, 4)] + [at_y(d) for d in range(1, 4)]
    partners += [device for device, _ in after + before]
    for device in partners:
        pl.semaphore_signal(barrier, inc=1, device_id=device, device_id_type=MESH)

    sub = lax.broadcasted_iota(jnp.int32, (128, 128), 0)
    lane = lax.broadcasted_iota(jnp.int32, (128, 128), 1)
    eye = sub == lane

    def to_col(row):
        return jnp.sum(jnp.where(eye, row, 0.0), axis=1, keepdims=True)

    def to_row(col):
        return jnp.sum(jnp.where(eye, col, 0.0), axis=0, keepdims=True)

    def block_of(b):
        return (y * 2 + lax.div(b, 2)) * 8 + x * 2 + lax.rem(b, 2)

    for b in range(4):
        vi[b] = to_col(vid_ref[pl.ds(block_of(b), 1), :])
    segment = lax.div(lax.broadcasted_iota(jnp.int32, (1, 128), 1), 16)
    for h in range(2):
        for grp in range(2):
            out = jnp.zeros((1, 128), F32)
            for s in range(8):
                a, b = grp * 2 + s // 4, s % 4
                ys, xs = (a, b) if h == 0 else (b, a)
                v = vid_ref[pl.ds((ys * 2 + zl) * 8 + xs * 2 + core, 1), :]
                shift = lax.rem(s * 16 + 256 - zh * 32 - h * 16, 128)
                out = jnp.where(segment == s, pltpu.roll(v, shift, 1), out)
            vj[:, (h * 2 + grp) * 128:(h * 2 + grp + 1) * 128] = out

    pl.semaphore_wait(barrier, len(partners))

    pending = []
    for d in range(1, 4):
        to = lax.rem(zh + d, 4)
        rows = pl.ds(pl.multiple_of(to * 32, 32), 32)
        for i, (src, dst) in enumerate(((caps_ref, ta), (clips_ref, ca))):
            pending.append(
                copy(src.at[rows, :], dst.at[zh], a2a_s.at[i, d], a2a_r.at[i, d], (dp, to))
            )
    own = pl.ds(pl.multiple_of(zh * 32, 32), 32)
    ca[zh] = clips_ref[own, :]
    ta[zh] = caps_ref[own, :]

    def unit(parts, held, i):
        full = jnp.concatenate([parts[k].astype(F32) for k in range(4)], axis=1)
        length = jnp.sqrt(jnp.sum(full * full, axis=1, keepdims=True) + EPSILON)
        value = full / length
        held[...] = value
        hlen[i] = length
        return value.astype(BF16)

    for c in pending[0::2]:
        c.wait()
    u = unit(ta, hcap, 1)
    ct[0, y, x] = u[0:16]
    ct[1, x, y] = u[16:32]
    stage_a = []
    for d in (2, 1, 3):
        src = ct.at[0, y, x]
        stage_a.append(copy(src, src, p_s.at[0, d], p_r.at[0, d], at_x(d)))
        src = ct.at[1, x, y]
        stage_a.append(copy(src, src, p_s.at[1, d], p_r.at[1, d], at_y(d)))
    for c in pending[1::2]:
        c.wait()
    cl[mine] = unit(ca, hclip, 0)
    z_copies = []
    src = cl.at[mine]
    sib_copies = [copy(src, src, s_s.at[0], s_r.at[0], sibling)]
    for d in (4, 3, 5, 2, 6, 1, 7):
        z_copies.append((d, copy(src, src, z_s.at[d], z_r.at[d], at_z(d))))
    for c in stage_a:
        c.wait()
    stage_b = []
    for d in (2, 1, 3):
        src = ct.at[0, y]
        stage_b.append(copy(src, src, p_s.at[2, d], p_r.at[2, d], at_y(d)))
        src = ct.at[1, x]
        stage_b.append(copy(src, src, p_s.at[3, d], p_r.at[3, d], at_x(d)))
    for d, c in sorted(z_copies, key=lambda t: min(t[0], 8 - t[0])):
        c.wait()
        zs = lax.rem(z + 8 - d, 8)
        src = cl.at[lax.rem(zs, 2) * 8 + core * 4 + lax.div(zs, 2)]
        sib_copies.append(copy(src, src, s_s.at[d], s_r.at[d], sibling))
    for c in sib_copies:
        c.wait()

    edge_copies = []
    for r in range(2):
        units = cl[8 * r:8 * r + 8].reshape(256, 768)
        ids = jnp.concatenate([vid_ref[pl.ds(block_of(2 * r + i), 1), :] for i in range(2)], axis=1)
        col = jnp.concatenate([vi[2 * r], vi[2 * r + 1]], axis=0)
        alike = jnp.where(col == ids, 1.0, 0.0).astype(BF16)
        local = jnp.dot(alike, units, preferred_element_type=F32)
        pu[2 * r] = local[0:128]
        pu[2 * r + 1] = local[128:256]
        eo[2 * r] = local[0:1]
        eo[2 * r + 1] = local[255:256]
        device, slot = before[r]
        edge_copies.append(
            copy(eo.at[2 * r], ei.at[slot * 2 + 1], e_s.at[2 * r], e_r.at[slot * 2 + 1], device)
        )
        device, slot = after[r]
        edge_copies.append(
            copy(eo.at[2 * r + 1], ei.at[slot * 2], e_s.at[2 * r + 1], e_r.at[slot * 2], device)
        )
    for c in stage_b:
        c.wait()

    scale = scale_ref[0]
    captions = ct[...].reshape(512, 768)
    sc[...] = lax.dot_general(
        cl[...].reshape(512, 768), captions, (((1,), (1,)), ((), ())), preferred_element_type=F32
    ).reshape(4, 128, 512)
    column = lax.broadcasted_iota(jnp.int32, (1, 512), 1)
    half = lax.div(column, 256)
    first = lax.rem(lax.div(column, 64), 4)
    second = lax.rem(lax.div(column, 16), 4)
    ypos = jnp.where(half == 0, first, second)
    xpos = jnp.where(half == 0, second, first)
    col_pos = ((ypos * 2 + zl) * 8 + xpos * 2 + core) * 128 + zh * 32 + half * 16
    col_pos = col_pos + lax.rem(column, 16)

    def pass_one(b, col_max):
        row_pos = block_of(b) * 128 + lax.broadcasted_iota(jnp.int32, (128, 1), 0)
        alike = vi[b] == vj[...]
        allowed = jnp.logical_not(alike) | (row_pos == col_pos)
        s = jnp.where(allowed, scale * sc[b], NEGATIVE_FILL)
        sc[b] = s
        same[b] = jnp.where(alike, 1.0, 0.0).astype(BF16)
        top = jnp.max(s, axis=1, keepdims=True)
        total = jnp.sum(jnp.exp(s - top), axis=1, keepdims=True)
        rst[pl.ds(b, 1), :] = to_row(top)
        rst[pl.ds(4 + b, 1), :] = to_row(total)
        return jnp.maximum(col_max, jnp.max(s, axis=0, keepdims=True))

    col_max = lax.fori_loop(0, 4, pass_one, jnp.full((1, 512), NEGATIVE_FILL, F32))
    stats = [copy(rst, rsib, t_s.at[0], t_r.at[0], sibling)]

    def pass_two(b, total):
        return total + jnp.sum(jnp.exp(sc[b] - col_max), axis=0, keepdims=True)

    col_sum = lax.fori_loop(0, 4, pass_two, jnp.zeros((1, 512), F32))
    for b in range(4):
        cst[b:b + 1, :] = col_max[:, b * 128:(b + 1) * 128]
        cst[4 + b:5 + b, :] = col_sum[:, b * 128:(b + 1) * 128]
    for d in (2, 1, 3):
        stats.append(copy(cst, cx.at[d], t_s.at[d], t_r.at[d], at_x(d)))

    edge_ids = []
    for r in range(2):
        q = runs[r]
        left = vid_ref[pl.ds(jnp.maximum(2 * q - 1, 0), 1), :][:, 127:128]
        right = vid_ref[pl.ds(jnp.minimum(2 * q + 2, 63), 1), :][:, 0:1]
        edge_ids.append((left, right, jnp.where(q > 0, 1.0, 0.0), jnp.where(q < 31, 1.0, 0.0)))
    for c in edge_copies:
        c.wait()
    for b in range(4):
        r = b // 2
        left, right, has_left, has_right = edge_ids[r]
        from_left = jnp.where(vi[b] == left, has_left, 0.0)
        from_right = jnp.where(vi[b] == right, has_right, 0.0)
        pooled = pu[b] + from_left * ei[2 * r] + from_right * ei[2 * r + 1]
        length = jnp.sqrt(jnp.sum(pooled * pooled, axis=1, keepdims=True) + EPSILON)
        plen[b] = length
        pu[b] = pooled / length

    def joined(first, others):
        top, total = first
        for m, s in others:
            new = jnp.maximum(top, m)
            total = total * jnp.exp(top - new) + s * jnp.exp(m - new)
            top = new
        return top, total

    for c in stats:
        c.wait()
    top, total = joined((rst[0:4], rst[4:8]), [(rsib[0:4], rsib[4:8])])
    rcomb[0:4] = top
    rcomb[4:8] = total
    stats = [copy(rcomb, rz.at[d], u_s.at[0, d], u_r.at[0, d], at_z(d)) for d in (4, 3, 5, 2, 6, 1, 7)]
    row_pair = (top, total)
    top, total = joined((cst[0:4], cst[4:8]), [(cx[d, 0:4], cx[d, 4:8]) for d in range(1, 4)])
    ccomb[0:4] = top
    ccomb[4:8] = total
    stats += [copy(ccomb, cy.at[d], u_s.at[1, d], u_r.at[1, d], at_y(d)) for d in (2, 1, 3)]
    col_pair = (top, total)

    def projected(b, carry):
        acc = jnp.dot(same[b], ct[...].reshape(512, 768), preferred_element_type=F32)
        pool = pu[b]
        acc = acc - pool * jnp.sum(pool * acc, axis=1, keepdims=True)
        pj[b] = acc * (0.5 / plen[b])
        return carry

    lax.fori_loop(0, 4, projected, 0)

    for c in stats:
        c.wait()
    top, total = joined(row_pair, [(rz[d, 0:4], rz[d, 4:8]) for d in range(1, 8)])
    row_lse = top + jnp.log(total)
    top, total = joined(col_pair, [(cy[d, 0:4], cy[d, 4:8]) for d in range(1, 4)])
    col_lse = top + jnp.log(total)
    col_lse = jnp.concatenate([col_lse[b:b + 1] for b in range(4)], axis=1)
    rst[0:4] = row_lse

    def weigh(b, carry):
        rows = to_col(rst[pl.ds(b, 1), :])
        s = sc[b]
        w = 0.5 * (jnp.exp(s - rows) + jnp.exp(s - col_lse))
        w = w.astype(BF16)
        wt[b] = w
        part = jnp.dot(w, ct[...].reshape(512, 768), preferred_element_type=F32) - pj[b]
        pj[b] = part
        g[pl.ds(pl.multiple_of(4 * b, 4), 4)] = part.astype(BF16).reshape(4, 32, 768)
        return carry

    lax.fori_loop(0, 4, weigh, 0)
    sib_copies = []
    for r in range(2):
        src = g.at[pl.ds(pl.multiple_of(8 * r + 4 * (1 - core), 4), 4)]
        sib_copies.append(copy(src, sb.at[r], w_s.at[0, r], w_r.at[0, r], sibling))

    part = lax.dot_general(
        wt[...].reshape(512, 512), cl[...].reshape(512, 768), (((0,), (0,)), ((), ())),
        preferred_element_type=F32,
    ).reshape(2, 4, 4, 16, 768)
    pc[...] = part
    g2[...] = part.astype(BF16)
    stage_a = []
    for d in (2, 1, 3):
        src = g2.at[0, lax.rem(y + d, 4)]
        stage_a.append(copy(src, qy.at[d], v_s.at[0, d], v_r.at[0, d], at_y(d)))
        src = g2.at[1, lax.rem(x + d, 4)]
        stage_a.append(copy(src, qx.at[d], v_s.at[1, d], v_r.at[1, d], at_x(d)))

    for c in sib_copies:
        c.wait()
    for r in range(2):
        both = pj[2 * r + core].reshape(4, 32, 768) + sb[r].astype(F32)
        hown[r] = both
        hb[r] = both.astype(BF16)
    z_copies = []
    for d in (4, 3, 5, 2, 6, 1, 7):
        to = lax.rem(z + d, 8)
        src = hb.at[lax.rem(to, 2), lax.div(to, 2)]
        z_copies.append(copy(src, rzs.at[d], w_s.at[1, d], w_r.at[1, d], at_z(d)))

    for c in stage_a:
        c.wait()
    total = pc[0, y] + qy[1].astype(F32) + qy[2].astype(F32) + qy[3].astype(F32)
    r0[...] = total
    r0b[...] = total.astype(BF16)
    total = pc[1, x] + qx[1].astype(F32) + qx[2].astype(F32) + qx[3].astype(F32)
    r1[...] = total
    r1b[...] = total.astype(BF16)
    stage_b = []
    for d in (2, 1, 3):
        src = r0b.at[lax.rem(x + d, 4)]
        stage_b.append(copy(src, fx.at[d], v_s.at[2, d], v_r.at[2, d], at_x(d)))
        src = r1b.at[lax.rem(y + d, 4)]
        stage_b.append(copy(src, fy.at[d], v_s.at[3, d], v_r.at[3, d], at_y(d)))
    for c in stage_b:
        c.wait()

    low = r0[x] + fx[1].astype(F32) + fx[2].astype(F32) + fx[3].astype(F32)
    high = r1[y] + fy[1].astype(F32) + fy[2].astype(F32) + fy[3].astype(F32)
    acc = jnp.concatenate([low, high], axis=0)
    held = hcap[...]
    clip_held = hclip[...]
    clip_unit = clip_held.astype(BF16).astype(F32)
    cap_unit = held.astype(BF16).astype(F32)
    pool_unit = pu[zl * 2 + core, pl.ds(pl.multiple_of(zh * 32, 32), 32), :]
    grad = scale * acc - 0.5 * scale * clip_unit - 0.5 * scale * pool_unit
    dcap_ref[...] = (grad - held * jnp.sum(held * grad, axis=1, keepdims=True)) / hlen[1]

    for c in z_copies:
        c.wait()
    acc = hown[zl, zh]
    for d in range(1, 8):
        acc = acc + rzs[d].astype(F32)
    grad = scale * acc - 0.5 * scale * cap_unit
    dclip_ref[...] = (
        grad - clip_held * jnp.sum(clip_held * grad, axis=1, keepdims=True)
    ) / hlen[0]


def body(clips, captions, video_id, logit_scale):
    vmem = pl.BlockSpec(memory_space=pltpu.VMEM)
    dma = lambda *shape: pltpu.SemaphoreType.DMA(shape)
    out = jax.ShapeDtypeStruct((32, 768), F32)
    V = pltpu.VMEM
    ids = video_id.reshape(64, 128).astype(F32)
    return pl.pallas_call(
        kernel,
        out_shape=(out, out),
        in_specs=[pl.BlockSpec(memory_space=pltpu.SMEM), vmem, vmem, vmem],
        out_specs=(vmem, vmem),
        scratch_shapes=[
            V((4, 32, 192), BF16), V((4, 32, 192), BF16),
            V((32, 768), F32), V((32, 768), F32), V((2, 32, 1), F32),
            V((16, 32, 768), BF16), V((2, 4, 4, 16, 768), BF16),
            V((4, 128, 1), F32), V((1, 512), F32),
            V((4, 128, 768), F32), V((4, 128, 1), F32), V((4, 1, 768), F32), V((4, 1, 768), F32),
            V((4, 128, 512), F32), V((4, 128, 512), BF16), V((4, 128, 512), BF16),
            V((4, 128, 768), F32),
            V((8, 128), F32), V((8, 128), F32), V((8, 128), F32), V((8, 8, 128), F32),
            V((8, 128), F32), V((4, 8, 128), F32), V((8, 128), F32), V((4, 8, 128), F32),
            V((16, 32, 768), BF16), V((2, 4, 32, 768), BF16), V((2, 4, 32, 768), BF16),
            V((2, 4, 32, 768), F32), V((8, 32, 768), BF16),
            V((2, 4, 4, 16, 768), BF16), V((2, 4, 4, 16, 768), F32),
            V((4, 4, 16, 768), BF16), V((4, 4, 16, 768), BF16),
            V((4, 16, 768), F32), V((4, 16, 768), F32),
            V((4, 16, 768), BF16), V((4, 16, 768), BF16),
            V((4, 16, 768), BF16), V((4, 16, 768), BF16),
            dma(2, 4), dma(2, 4), dma(8), dma(8), dma(8), dma(8), dma(4, 4), dma(4, 4),
            dma(4), dma(4), dma(4), dma(4), dma(2, 8), dma(2, 8), dma(2, 8), dma(2, 8),
            dma(4, 4), dma(4, 4),
        ],
        compiler_params=pltpu.CompilerParams(
            collective_id=0, has_side_effects=True, vmem_limit_bytes=48 * 1024 * 1024
        ),
        name="contrastive",
    )(logit_scale.reshape(1), ids, clips, captions)


def solution(mesh):
    in_specs = (P("dp", "mp"), P("dp", "mp"), P(), P())
    out_specs = (P(("dp", "mp"), None), P(("dp", "mp"), None))
    return jax.shard_map(body, mesh=mesh, in_specs=in_specs, out_specs=out_specs, check_vma=False)
```

time: 1360 us -> 58.1 us (0.04)
  waiting for transfers between devices: 951 us -> 0 us
  matrix products: 164 us -> 0 us
  local copies, waits for them, and re-layouts: 101 us -> 2.18 us
  starting transfers between devices: 56.4 us -> 0 us
  Pallas kernels: 0 us -> 53.6 us
  blocking collectives: 29.6 us -> 0 us
  other arithmetic: 21.9 us -> 0.76 us
  between operations: 15 us -> 1.32 us
  loops' own time: 13.6 us -> 0 us
    ppermute x383 -> x0, waiting for transfers between devices: 931 us -> none  [the longest x381 930 us: shifted(): return lax.ppermute(block, axis, route)]
    dot_general x321 -> x0, matrix products: 164 us -> none  [the longest x128 113 us: tile_scores(): lax.dot_general(caption_panel, clip_unit, (((1,), (1,)), ((), ())), prefe...]
    dynamic_slice x129 -> x0, local copies, waits for them, and re-layouts: 98.5 us -> none  [the longest x127 97 us: tile_masks(): panel_videos = lax.dynamic_slice_in_dim(video_id, first_row, sub_rows, 0)]
    pallas_call x0 -> x1, Pallas kernels: none -> 53.6 us  [body(): pl.pallas_call(kernel, out_shape=(out, out), in_specs=[pl.BlockSpec(memor...]
    ppermute x383 -> x0, starting transfers between devices: 47.3 us -> none  [the longest x381 38.5 us: shifted(): return lax.ppermute(block, axis, route)]
    all_gather x3 -> x0, blocking collectives: 29.6 us -> none  [the longest x2 15.9 us: combined_all(): everything = jax.tree.map(lambda part: lax.all_gather(part, axis), value)]
    reduce_scatter x1 -> x0, waiting for transfers between devices: 20 us -> none  [body(): lax.psum_scatter(partial_grad.astype(jnp.bfloat16), 'mp', scatter_dimensi...]
    reduce_sum x70 -> x0, other arithmetic: 13.9 us -> none  [the longest x63 11.8 us: forward_update(): col_sum = col_sum * jnp.exp(col_max - new_col) + jnp.sum(col_terms, axis=1)]
  transfers between devices with their start and end apart: 385 -> 0, of which waited for: 255 -> 0; matrix products, arithmetic and copies ran while one was open for 21% -> 0% of each run, Pallas kernels for 0% -> 0%
where the time goes in v1:
time: 58.1 us; the launch traced here: 57.9 us
  Pallas kernels  53.6 us (92%)
  local copies, waits for them, and re-layouts  2.18 us (4%)
  between operations  1.32 us (2%)
  other arithmetic  0.76 us (1%)
    pallas_call x1, Pallas kernels, body(): pl.pallas_call(kernel, out_shape=(out, out), in_specs=[pl.BlockSpec(memor...  53.6 us
    unnamed x8, local copies, waits for them, and re-layouts  2.18 us

profile of v1, /device:TPU:1, one launch (start us, length us, event | category | flops | bytes accessed | tf_op | source)
XLA Modules:
  0.0 57.9 jit_solution(11657128254519828737)
XLA Ops:
  0.6 0.0 copy-start
  1.3 0.8 %convert_bitcast_fusion.vid_ref = f32[64,128]{1,0:T(8,128)S(1)} fusion(s32[8192]{0:T(1024)} %param.6), kind=kLoop, calls=%fused_computation | loop fusion | flops 8192 | bytes 65536 | tf_op jit(solution)/shard_map/convert_element_type | solution.py:357
  2.1 0.0 copy-done
  2.1 0.0 copy-start.1
  2.1 0.1 copy.6.clips_ref
  2.2 0.7 %copy-done.1 = bf16[128,192]{0,1:T(8,128)(2,1)S(1)} copy-done((bf16[128,192]{0,1:T(8,128)(2,1)S(1)}, bf16[128,192]{0,1:T(8,128)(2,1)}, u32[]{:S(2)}) %copy-start.1) | copy-done | bytes 49176
  2.9 0.1 copy.7.caps_ref
  3.0 53.6 %contrastive.1 = (f32[32,768]{1,0:T(8,128)S(1)}, f32[32,768]{1,0:T(8,128)S(1)}) custom-call(f32[1]{0:T(128)} %bitcast.3.scale_ref, f32[64,128]{1,0:T(8,128)S(1)} %convert_bitcast_fusion.vid_ref, bf16[128,192]{1,0:T(8,128)(2,1)S(1)} %copy.6.clips_ref, bf16[128,192]{1,0:T(8,128)(2,1)S(1)} %copy.7.caps_ref), custom_call_target="tpu_custom_call" | custom-call | tf_op jit(solution)/shard_map/contrastive/pallas_call | solution.py:358
  56.6 0.6 %copy.11 = f32[32,768]{1,0:T(8,128)} copy(f32[32,768]{1,0:T(8,128)S(1)} %get-tuple-element.4) | data formatting | bytes 196608
  57.3 0.6 %copy.12 = f32[32,768]{1,0:T(8,128)} copy(f32[32,768]{1,0:T(8,128)S(1)} %get-tuple-element.5) | data formatting | bytes 196608
Async XLA Ops:
  0.6 1.4 %copy-start = (bf16[128,192]{0,1:T(8,128)(2,1)S(1)}, bf16[128,192]{0,1:T(8,128)(2,1)}, u32[]{:S(2)}) copy-start(bf16[128,192]{0,1:T(8,128)(2,1)} %param.4) | copy-start | bytes 147460
  2.1 0.8 %copy-start.1 = (bf16[128,192]{0,1:T(8,128)(2,1)S(1)}, bf16[128,192]{0,1:T(8,128)(2,1)}, u32[]{:S(2)}) copy-start(bf16[128,192]{0,1:T(8,128)(2,1)} %param.5) | copy-start | bytes 147460

commit v2 on v1

v2 whole, which is shorter than its diff:
```python
import jax
import jax.numpy as jnp
from jax import lax
from jax.experimental import pallas as pl
from jax.experimental.pallas import tpu as pltpu
from jax.sharding import PartitionSpec as P

EPSILON = 1e-06
NEGATIVE_FILL = -1e30
F32 = jnp.float32
BF16 = jnp.bfloat16
MESH = pl.DeviceIdType.MESH


def chip(x, y, z, core):
    return ((y * 2 + lax.rem(z, 2)) * 8 + x * 2 + core, lax.div(z, 2))


def kernel(
    scale_ref, vid_ref, clips_ref, caps_ref,
    dclip_ref, dcap_ref,
    raw, vid, pkt, ta, cr, hcap, hclip, hlen,
    clt, ct, vic, vjr, vir, vjc,
    pu, plen, eo, ei,
    ej, ek, ejt, ekt, pj,
    rst, rz, cst, cz,
    g, sb, hb, hown, rzs,
    pc, g2, got,
    l_s, a2a_s, a2a_r, z_s, z_r, s_s, s_r, p_s, p_r, e_s, e_r,
    t_s, t_r, w_s, w_r, v_s, v_r,
):
    dp = lax.axis_index("dp")
    zh = lax.axis_index("mp")
    core = lax.rem(dp, 2)
    x = lax.rem(lax.div(dp, 2), 4)
    zl = lax.rem(lax.div(dp, 8), 2)
    y = lax.div(dp, 16)
    z = zh * 2 + zl
    home = zl * 2 + core
    sibling = chip(x, y, z, 1 - core)
    at_z = lambda d: chip(x, y, lax.rem(z + d, 8), core)
    at_xy = lambda i, j: chip(lax.rem(x + i, 4), lax.rem(y + j, 4), z, core)
    others_z = (4, 3, 5, 2, 6, 1, 7)
    others_xy = sorted(
        [(i, j) for i in range(4) for j in range(4) if i or j],
        key=lambda t: -(min(t[0], 4 - t[0]) + min(t[1], 4 - t[1])),
    )

    def copy(src, dst, send, recv, device):
        c = pltpu.make_async_remote_copy(
            src_ref=src, dst_ref=dst, send_sem=send, recv_sem=recv,
            device_id=device, device_id_type=MESH,
        )
        c.start()
        return c

    runs = [y * 8 + x, y * 8 + 4 + x]

    def owner(q):
        return chip(lax.rem(q, 4), lax.div(q, 8), z, core), lax.rem(lax.div(q, 4), 2)

    after = [owner(lax.rem(q + 1, 32)) for q in runs]
    before = [owner(lax.rem(q + 31, 32)) for q in runs]

    barrier = pltpu.get_barrier_semaphore()
    partners = [at_z(d) for d in others_z]
    partners += [chip(x, y, lax.rem(z + d, 8), 1 - core) for d in others_z]
    partners += [at_xy(i, j) for i, j in others_xy] + [sibling]
    for device in partners:
        pl.semaphore_signal(barrier, inc=1, device_id=device, device_id_type=MESH)
    loads = [
        pltpu.make_async_copy(src, dst, l_s.at[i])
        for i, (src, dst) in enumerate(((caps_ref, raw.at[1]), (clips_ref, raw.at[0]), (vid_ref, vid)))
    ]
    for c in loads:
        c.start()

    loads[0].wait()
    block = raw[1].astype(F32).T
    for k in range(4):
        pkt[k, 0:32] = block[32 * k:32 * k + 32, 0:128].astype(BF16)
        tail = block[32 * k:32 * k + 32, 128:192]
        pkt[k, 32:48] = jnp.concatenate([tail[0:16], tail[16:32]], axis=1).astype(BF16)
    ta[zh] = pkt[zh]
    loads[1].wait()
    slot = lambda at, c: lax.rem(at, 2) * 8 + c * 4 + lax.div(at, 2)
    mine = slot(z, core)
    cr[mine] = raw[0]

    loads[2].wait()
    sub = lax.broadcasted_iota(jnp.int32, (128, 128), 0)
    lane = lax.broadcasted_iota(jnp.int32, (128, 128), 1)
    eye = sub == lane

    def to_col(row):
        return jnp.sum(jnp.where(eye, row, 0.0), axis=1, keepdims=True)

    def to_row(col):
        return jnp.sum(jnp.where(eye, col, 0.0), axis=0, keepdims=True)

    def block_of(b):
        return (y * 2 + lax.div(b, 2)) * 8 + x * 2 + lax.rem(b, 2)

    def ids_of(row):
        return vid[pl.ds(row, 1), :].astype(F32)

    for b in range(4):
        ids = ids_of(block_of(b))
        vir[:, 128 * b:128 * b + 128] = ids
        vic[b] = to_col(ids)
    segment = lax.div(lax.broadcasted_iota(jnp.int32, (1, 128), 1), 32)
    for b in range(4):
        out = jnp.zeros((1, 128), F32)
        for i in range(4):
            v = ids_of((b * 2 + zl) * 8 + i * 2 + core)
            out = jnp.where(segment == i, pltpu.roll(v, lax.rem((i + 4 - zh) * 32, 128), 1), out)
        vjr[:, 128 * b:128 * b + 128] = out
        vjc[b] = to_col(out)

    pl.semaphore_wait(barrier, len(partners))

    pending = []
    for d in (2, 1, 3):
        to = lax.rem(zh + d, 4)
        pending.append(copy(pkt.at[to], ta.at[zh], a2a_s.at[d], a2a_r.at[d], (dp, to)))
    own = raw.at[0]
    sib_copies = [copy(own, cr.at[mine], s_s.at[0], s_r.at[0], sibling)]
    z_copies = [
        (d, copy(own, cr.at[mine], z_s.at[d], z_r.at[d], at_z(d))) for d in others_z
    ]

    def unpacked(parts):
        low = lax.broadcasted_iota(jnp.int32, (16, 128), 1) < 64
        tiles = [p[0:32].astype(F32) for p in parts]
        tails = [p[32:48].astype(F32) for p in parts]
        for i in (0, 2):
            left, right = tails[i], tails[i + 1]
            upper = jnp.where(low, left, pltpu.roll(right, 64, 1))
            lower = jnp.where(low, pltpu.roll(left, 64, 1), right)
            tiles.append(jnp.concatenate([upper, lower], axis=0))
        return jnp.concatenate(tiles, axis=1)

    def lengths(full):
        return jnp.sqrt(jnp.sum(full * full, axis=1, keepdims=True) + EPSILON)

    for c in pending:
        c.wait()
    full = unpacked([ta[k] for k in range(4)])
    length = lengths(full)
    full = full / length
    hcap[...] = full
    hlen[1] = length
    u = full.astype(BF16)
    at = y * 4 + x
    ct[at] = u
    plane = []
    for i, j in others_xy:
        ref = ct.at[at]
        plane.append(copy(ref, ref, p_s.at[i, j], p_r.at[i, j], at_xy(i, j)))
    for d, c in z_copies:
        c.wait()
        ref = cr.at[slot(lax.rem(z + 8 - d, 8), core)]
        sib_copies.append(copy(ref, ref, s_s.at[d], s_r.at[d], sibling))
    for c in sib_copies:
        c.wait()

    def normalise(b, carry):
        parts = [cr[4 * b + k].astype(F32) for k in range(4)]
        total = sum(jnp.sum(p * p, axis=0, keepdims=True) for p in parts)
        inverse = 1.0 / jnp.sqrt(total + EPSILON)
        columns = pl.ds(pl.multiple_of(128 * b, 128), 128)
        for k, p in enumerate(parts):
            p = (p * inverse).astype(BF16)
            clt[128 * k:128 * k + 128, columns] = p[0:128]
            clt[512 + 64 * k:576 + 64 * k, columns] = p[128:192]
        return carry

    lax.fori_loop(0, 4, normalise, 0)
    for c in plane:
        c.wait()

    scale = scale_ref[0]
    ej[...] = jnp.dot(
        ct[...].reshape(512, 768), clt[...], preferred_element_type=F32
    ).reshape(4, 128, 512)
    column = lax.broadcasted_iota(jnp.int32, (1, 512), 1)
    clip_pos = (y * 2 + lax.div(column, 256)) * 1024 + x * 256 + lax.rem(column, 256)

    def pass_one(b, top):
        j = b * 128 + lax.broadcasted_iota(jnp.int32, (128, 1), 0)
        cap_pos = ((b * 2 + zl) * 8 + lax.rem(lax.div(j, 32), 4) * 2 + core) * 128
        cap_pos = cap_pos + zh * 32 + lax.rem(j, 32)
        alike = vjc[b] == vir[...]
        allowed = jnp.logical_not(alike) | (cap_pos == clip_pos)
        s = jnp.where(allowed, scale * ej[b], NEGATIVE_FILL)
        ej[b] = s
        return jnp.maximum(top, jnp.max(s, axis=0, keepdims=True))

    clip_top = lax.fori_loop(0, 4, pass_one, jnp.full((1, 512), NEGATIVE_FILL, F32))

    def pass_two(b, total):
        e = jnp.exp(ej[b] - clip_top)
        ek[b] = e
        return total + jnp.sum(e, axis=0, keepdims=True)

    clip_sum = lax.fori_loop(0, 4, pass_two, jnp.zeros((1, 512), F32))
    for b in range(4):
        rst[b:b + 1, :] = clip_top[:, b * 128:(b + 1) * 128]
        rst[4 + b:5 + b, :] = clip_sum[:, b * 128:(b + 1) * 128]
    stats = []
    for d in others_z + (0,):
        for i in range(2):
            if d or i:
                n = i * 8 + d
                device = chip(x, y, lax.rem(z + d, 8), core if i == 0 else 1 - core)
                stats.append(copy(rst, rz.at[n], t_s.at[0, n], t_r.at[0, n], device))

    def pass_three(b, carry):
        s = ej[b]
        top = jnp.max(s, axis=1, keepdims=True)
        e = jnp.exp(s - top)
        ej[b] = e
        cst[pl.ds(b, 1), :] = to_row(top)
        cst[pl.ds(4 + b, 1), :] = to_row(jnp.sum(e, axis=1, keepdims=True))
        return carry

    lax.fori_loop(0, 4, pass_three, 0)
    for i, j in others_xy:
        n = i * 4 + j
        stats.append(copy(cst, cz.at[n], t_s.at[1, n], t_r.at[1, n], at_xy(i, j)))
    rz[0] = rst[...]
    cz[0] = cst[...]

    def joined(ref):
        tops = ref[:, 0:4]
        top = jnp.max(tops, axis=0)
        return top + jnp.log(jnp.sum(ref[:, 4:8] * jnp.exp(tops - top), axis=0))

    edge_copies = []
    for r in range(2):
        ids = vir[:, 256 * r:256 * r + 256]
        col = jnp.concatenate([vic[2 * r], vic[2 * r + 1]], axis=0)
        alike = jnp.where(col == ids, 1.0, 0.0).astype(BF16)
        local = lax.dot_general(
            alike, clt[:, 256 * r:256 * r + 256], (((1,), (1,)), ((), ())),
            preferred_element_type=F32,
        )
        pu[2 * r] = local[0:128]
        pu[2 * r + 1] = local[128:256]
        eo[2 * r] = local[0:1]
        eo[2 * r + 1] = local[255:256]
        device, side = before[r]
        edge_copies.append(
            copy(eo.at[2 * r], ei.at[side * 2 + 1], e_s.at[2 * r], e_r.at[side * 2 + 1], device)
        )
        device, side = after[r]
        edge_copies.append(
            copy(eo.at[2 * r + 1], ei.at[side * 2], e_s.at[2 * r + 1], e_r.at[side * 2], device)
        )

    for b in range(4):
        ejt[:, b * 128:(b + 1) * 128] = ej[b].T
        ekt[:, b * 128:(b + 1) * 128] = ek[b].T
    parts = [cr[4 * home + k].astype(F32) for k in range(4)]
    full = jnp.concatenate([p[0:128] for p in parts] + [p[128:192] for p in parts], axis=0)
    pj[0] = full.T
    rows = pl.ds(pl.multiple_of(zh * 32, 32), 32)
    full = pj[0, rows, :]
    length = lengths(full)
    hclip[...] = full / length
    hlen[0] = length
    for c in edge_copies:
        c.wait()
    for b in range(4):
        r = b // 2
        q = runs[r]
        left = ids_of(jnp.maximum(2 * q - 1, 0))[:, 127:128]
        right = ids_of(jnp.minimum(2 * q + 2, 63))[:, 0:1]
        from_left = jnp.where(vic[b] == left, jnp.where(q > 0, 1.0, 0.0), 0.0)
        from_right = jnp.where(vic[b] == right, jnp.where(q < 31, 1.0, 0.0), 0.0)
        pooled = pu[b] + from_left * ei[2 * r] + from_right * ei[2 * r + 1]
        length = lengths(pooled)
        plen[b] = length
        pu[b] = pooled * (1.0 / length)

    def projected(b, carry):
        alike = jnp.where(vic[b] == vjr[...], 1.0, 0.0).astype(BF16)
        acc = jnp.dot(alike, ct[...].reshape(512, 768), preferred_element_type=F32)
        pool = pu[b]
        acc = acc - pool * jnp.sum(pool * acc, axis=1, keepdims=True)
        pj[b] = acc * (0.5 / plen[b])
        return carry

    lax.fori_loop(0, 4, projected, 0)

    for c in stats:
        c.wait()
    clip_fac = 0.5 * jnp.exp(rst[0:4] - joined(rz))
    cap_fac = 0.5 * jnp.exp(cst[0:4] - joined(cz))
    clip_line = jnp.concatenate([clip_fac[b:b + 1] for b in range(4)], axis=1)
    cap_line = jnp.concatenate([cap_fac[b:b + 1] for b in range(4)], axis=1)
    rst[0:4] = clip_fac
    cst[0:4] = cap_fac

    def weigh(c):
        blocks = [c, 2 + c]
        w = []
        for b in blocks:
            rows = pl.ds(pl.multiple_of(128 * b, 128), 128)
            w.append(
                (ekt[rows, :] * to_col(rst[pl.ds(b, 1), :]) + ejt[rows, :] * cap_line).astype(BF16)
            )
        part = jnp.dot(
            jnp.concatenate(w, axis=0), ct[...].reshape(512, 768), preferred_element_type=F32
        )
        return [part[128 * i:128 * i + 128] - pj[b] for i, b in enumerate(blocks)]

    sib_copies = []
    for r, part in enumerate(weigh(1 - core)):
        g[r] = part.astype(BF16).reshape(4, 32, 768)
        sib_copies.append(copy(g.at[r], sb.at[r], w_s.at[0, r], w_r.at[0, r], sibling))
    for r, part in enumerate(weigh(core)):
        hown[r] = part.reshape(4, 32, 768)


    back = []

    def caption_part(offsets):
        blocks = [lax.rem(y + j, 4) for j in offsets]
        w = [
            (ek[b] * clip_line + ej[b] * to_col(cst[pl.ds(b, 1), :])).astype(BF16) for b in blocks
        ]
        part = lax.dot_general(
            jnp.concatenate(w, axis=0), clt[...], (((1,), (1,)), ((), ())),
            preferred_element_type=F32,
        ).reshape(2, 4, 32, 768)
        for n, j in enumerate(offsets):
            g2[j] = part[n].astype(BF16)
            if j == 0:
                pc[...] = part[n]
            for i in (2, 1, 3, 0):
                if i or j:
                    src = g2.at[j, lax.rem(x + i, 4)]
                    back.append(
                        copy(src, got.at[i * 4 + j], v_s.at[i, j], v_r.at[i, j], at_xy(i, j))
                    )

    caption_part((2, 1))
    z_copies = []
    for c in sib_copies:
        c.wait()
    for r in range(2):
        both = hown[r] + sb[r].astype(F32)
        hown[r] = both
        hb[r] = both.astype(BF16)
    for d in others_z:
        to = lax.rem(z + d, 8)
        src = hb.at[lax.rem(to, 2), lax.div(to, 2)]
        z_copies.append(copy(src, rzs.at[d], w_s.at[1, d], w_r.at[1, d], at_z(d)))
    caption_part((3, 0))
    for c in back:
        c.wait()

    def ordered(v):
        tiles = [v[:, 128 * i:128 * i + 128] for i in range(4)]
        tails = [v[:, 512 + 64 * i:576 + 64 * i] for i in range(4)]
        return jnp.concatenate([t for pair in zip(tiles, tails) for t in pair], axis=1)

    acc = pc[x]
    for n in range(1, 16):
        acc = acc + got[n].astype(F32)
    held = hcap[...]
    clip_held = hclip[...]
    clip_unit = clip_held.astype(BF16).astype(F32)
    cap_unit = held.astype(BF16).astype(F32)
    pool_unit = pu[home, rows, :]
    grad = scale * acc - 0.5 * scale * clip_unit - 0.5 * scale * pool_unit
    dcap_ref[...] = ordered(
        (grad - held * jnp.sum(held * grad, axis=1, keepdims=True)) / hlen[1]
    )

    for c in z_copies:
        c.wait()
    acc = hown[zl, zh]
    for d in range(1, 8):
        acc = acc + rzs[d].astype(F32)
    grad = scale * acc - 0.5 * scale * cap_unit
    dclip_ref[...] = ordered(
        (grad - clip_held * jnp.sum(clip_held * grad, axis=1, keepdims=True)) / hlen[0]
    )


def body(clips, captions, video_id, logit_scale):
    vmem = pl.BlockSpec(memory_space=pltpu.VMEM)
    hbm = pl.BlockSpec(memory_space=pltpu.HBM)
    dma = lambda *shape: pltpu.SemaphoreType.DMA(shape)
    out = jax.ShapeDtypeStruct((32, 768), F32)
    V = pltpu.VMEM
    keep = lambda v: pltpu.with_memory_space_constraint(v, pltpu.HBM)
    return pl.pallas_call(
        kernel,
        out_shape=(out, out),
        in_specs=[pl.BlockSpec(memory_space=pltpu.SMEM), hbm, hbm, hbm],
        out_specs=(vmem, vmem),
        scratch_shapes=[
            V((2, 192, 128), BF16), V((64, 128), jnp.int32),
            V((4, 48, 128), BF16), V((4, 48, 128), BF16), V((16, 192, 128), BF16),
            V((32, 768), F32), V((32, 768), F32), V((2, 32, 1), F32),
            V((768, 512), BF16), V((16, 32, 768), BF16),
            V((4, 128, 1), F32), V((1, 512), F32), V((1, 512), F32), V((4, 128, 1), F32),
            V((4, 128, 768), F32), V((4, 128, 1), F32), V((4, 1, 768), F32), V((4, 1, 768), F32),
            V((4, 128, 512), F32), V((4, 128, 512), F32), V((512, 512), F32), V((512, 512), F32),
            V((4, 128, 768), F32),
            V((8, 128), F32), V((16, 8, 128), F32), V((8, 128), F32), V((16, 8, 128), F32),
            V((2, 4, 32, 768), BF16), V((2, 4, 32, 768), BF16), V((2, 4, 32, 768), BF16),
            V((2, 4, 32, 768), F32), V((8, 32, 768), BF16),
            V((4, 32, 768), F32), V((4, 4, 32, 768), BF16), V((16, 32, 768), BF16),
            dma(3), dma(4), dma(4), dma(8), dma(8), dma(8), dma(8), dma(4, 4), dma(4, 4),
            dma(4), dma(4), dma(2, 16), dma(2, 16), dma(2, 8), dma(2, 8), dma(4, 4), dma(4, 4),
        ],
        compiler_params=pltpu.CompilerParams(
            collective_id=0, has_side_effects=True, vmem_limit_bytes=48 * 1024 * 1024
        ),
        name="contrastive",
    )(logit_scale.reshape(1), keep(video_id.reshape(64, 128)), keep(clips.T), keep(captions.T))


def solution(mesh):
    in_specs = (P("dp", "mp"), P("dp", "mp"), P(), P())
    out_specs = (P(("dp", "mp"), None), P(("dp", "mp"), None))
    return jax.shard_map(body, mesh=mesh, in_specs=in_specs, out_specs=out_specs, check_vma=False)
```

time: 58.1 us -> 53.8 us (0.926)
  Pallas kernels: 53.6 us -> 51 us
  local copies, waits for them, and re-layouts: 2.18 us -> 1.28 us
  other arithmetic: 0.76 us -> 0 us
    pallas_call x1, Pallas kernels: 53.6 us -> 51 us  [body(): pl.pallas_call(kernel, out_shape=(out, out), in_specs=[pl.BlockSpec(memor...]
    unnamed x8 -> x2, local copies, waits for them, and re-layouts: 2.18 us -> 1.28 us
    convert_element_type x1 -> x0, other arithmetic: 0.76 us -> none  [body(): ids = video_id.reshape(64, 128).astype(F32)]
where the time goes in v2:
time: 53.8 us; the launch traced here: 53.6 us
  Pallas kernels  51 us (95%)
  between operations  1.29 us (2%)
  local copies, waits for them, and re-layouts  1.28 us (2%)
    pallas_call x1, Pallas kernels, body(): pl.pallas_call(kernel, out_shape=(out, out), in_specs=[pl.BlockSpec(memor...  51 us
    unnamed x2, local copies, waits for them, and re-layouts  1.28 us

profile of v2, /device:TPU:1, one launch (start us, length us, event | category | flops | bytes accessed | tf_op | source)
XLA Modules:
  0.0 53.6 jit_solution(13182129357766873398)
XLA Ops:
  1.3 51.0 %contrastive.1 = (f32[32,768]{1,0:T(8,128)S(1)}, f32[32,768]{1,0:T(8,128)S(1)}) custom-call(f32[1]{0:T(128)} %bitcast.4.scale_ref, s32[64,128]{1,0:T(8,128)} %bitcast.7, bf16[192,128]{1,0:T(8,128)(2,1)} %bitcast.5, bf16[192,128]{1,0:T(8,128)(2,1)} %bitcast.6), custom_call_target="tpu_custom_call" | custom-call | tf_op jit(solution)/shard_map/contrastive/pallas_call | solution.py:400
  52.3 0.6 %copy.9 = f32[32,768]{1,0:T(8,128)} copy(f32[32,768]{1,0:T(8,128)S(1)} %get-tuple-element.4) | data formatting | bytes 196608
  53.0 0.6 %copy.10 = f32[32,768]{1,0:T(8,128)} copy(f32[32,768]{1,0:T(8,128)S(1)} %get-tuple-element.5) | data formatting | bytes 196608

commit v3 on v2

--- a/solution.py
+++ b/solution.py
@@ -22,12 +22,12 @@
     raw, vid, pkt, ta, cr, hcap, hclip, hlen,
     clt, ct, vic, vjr, vir, vjc,
     pu, plen, eo, ei,
-    ej, ek, ejt, ekt, pj,
+    ej, ek, ejt, ekt, pj, ctop,
     rst, rz, cst, cz,
-    g, sb, hb, hown, rzs,
-    pc, g2, got,
-    l_s, a2a_s, a2a_r, z_s, z_r, s_s, s_r, p_s, p_r, e_s, e_r,
-    t_s, t_r, w_s, w_r, v_s, v_r,
+    g, sb, hb, hown, s1, s1h, m1, m2, r1z, r2z,
+    g2, pc, qy, qx, r0, r1, r0b, r1b, fx, fy,
+    l_s, a2a_s, a2a_r, z_s, z_r, s_s, s_r, p_s, p_r, f_s, f_r, e_s, e_r,
+    t_s, t_r, w_s, w_r, x_s, x_r, v_s, v_r,
 ):
     dp = lax.axis_index("dp")
     zh = lax.axis_index("mp")
@@ -39,12 +39,15 @@
     home = zl * 2 + core
     sibling = chip(x, y, z, 1 - core)
     at_z = lambda d: chip(x, y, lax.rem(z + d, 8), core)
-    at_xy = lambda i, j: chip(lax.rem(x + i, 4), lax.rem(y + j, 4), z, core)
+    at_x = lambda d: chip(lax.rem(x + d, 4), y, z, core)
+    at_y = lambda d: chip(x, lax.rem(y + d, 4), z, core)
+
     others_z = (4, 3, 5, 2, 6, 1, 7)
     others_xy = sorted(
         [(i, j) for i in range(4) for j in range(4) if i or j],
         key=lambda t: -(min(t[0], 4 - t[0]) + min(t[1], 4 - t[1])),
     )
+    at_xy = lambda i, j: chip(lax.rem(x + i, 4), lax.rem(y + j, 4), z, core)
 
     def copy(src, dst, send, recv, device):
         c = pltpu.make_async_remote_copy(
@@ -108,14 +111,18 @@
         ids = ids_of(block_of(b))
         vir[:, 128 * b:128 * b + 128] = ids
         vic[b] = to_col(ids)
-    segment = lax.div(lax.broadcasted_iota(jnp.int32, (1, 128), 1), 32)
-    for b in range(4):
-        out = jnp.zeros((1, 128), F32)
-        for i in range(4):
-            v = ids_of((b * 2 + zl) * 8 + i * 2 + core)
-            out = jnp.where(segment == i, pltpu.roll(v, lax.rem((i + 4 - zh) * 32, 128), 1), out)
-        vjr[:, 128 * b:128 * b + 128] = out
-        vjc[b] = to_col(out)
+    segment = lax.div(lax.broadcasted_iota(jnp.int32, (1, 128), 1), 16)
+    for h in range(2):
+        for grp in range(2):
+            out = jnp.zeros((1, 128), F32)
+            for s in range(8):
+                a, b = grp * 2 + s // 4, s % 4
+                ys, xs = (a, b) if h == 0 else (b, a)
+                v = ids_of((ys * 2 + zl) * 8 + xs * 2 + core)
+                shift = lax.rem(s * 16 + 256 - zh * 32 - h * 16, 128)
+                out = jnp.where(segment == s, pltpu.roll(v, shift, 1), out)
+            vjr[:, (h * 2 + grp) * 128:(h * 2 + grp + 1) * 128] = out
+            vjc[h * 2 + grp] = to_col(out)
 
     pl.semaphore_wait(barrier, len(partners))
 
@@ -125,9 +132,23 @@
         pending.append(copy(pkt.at[to], ta.at[zh], a2a_s.at[d], a2a_r.at[d], (dp, to)))
     own = raw.at[0]
     sib_copies = [copy(own, cr.at[mine], s_s.at[0], s_r.at[0], sibling)]
-    z_copies = [
-        (d, copy(own, cr.at[mine], z_s.at[d], z_r.at[d], at_z(d))) for d in others_z
-    ]
+    near = {d: copy(own, cr.at[mine], z_s.at[d], z_r.at[d], at_z(d)) for d in (1, 7, 2, 6)}
+
+    def to_sibling(d):
+        ref = cr.at[slot(lax.rem(z + 8 - d, 8), core)]
+        sib_copies.append(copy(ref, ref, s_s.at[d], s_r.at[d], sibling))
+
+    far = {}
+
+    def relay(d, to, sem, rows):
+        near[d].wait()
+        at = slot(lax.rem(z + 8 - d, 8), core)
+        ref = cr.at[at] if rows is None else cr.at[at, pl.ds(rows, 96)]
+        far[sem] = copy(ref, ref, z_s.at[sem], z_r.at[sem], at_z(to))
+        to_sibling(d)
+
+    relay(1, 2, 3, None)
+    relay(7, 6, 5, None)
 
     def unpacked(parts):
         low = lax.broadcasted_iota(jnp.int32, (16, 128), 1) < 64
@@ -151,16 +172,37 @@
     hcap[...] = full
     hlen[1] = length
     u = full.astype(BF16)
-    at = y * 4 + x
-    ct[at] = u
-    plane = []
-    for i, j in others_xy:
-        ref = ct.at[at]
-        plane.append(copy(ref, ref, p_s.at[i, j], p_r.at[i, j], at_xy(i, j)))
-    for d, c in z_copies:
-        c.wait()
-        ref = cr.at[slot(lax.rem(z + 8 - d, 8), core)]
-        sib_copies.append(copy(ref, ref, s_s.at[d], s_r.at[d], sibling))
+    ct[0, y, x] = u[0:16]
+    ct[1, x, y] = u[16:32]
+    axes = ((at_x, at_y, y, x), (at_y, at_x, x, y))
+    stage_a = [[], []]
+    for d in (2, 1, 3):
+        for h, (along, _, i, j) in enumerate(axes):
+            ref = ct.at[h, i, j]
+            stage_a[h].append((d, copy(ref, ref, p_s.at[h, d], p_r.at[h, d], along(d))))
+    stage_b = []
+
+    def forward(h, e):
+        _, across, i, j = axes[h]
+        ref = ct.at[h, i, lax.rem(j + 4 - e, 4)]
+        for d in (2, 1, 3):
+            stage_b.append(copy(ref, ref, f_s.at[h, e, d], f_r.at[h, e, d], across(d)))
+
+    forward(0, 0)
+    forward(1, 0)
+    relay(2, 2, 4, 0)
+    relay(6, 6, 0, 96)
+    for n in (1, 2, 0):
+        for h in range(2):
+            d, c = stage_a[h][n]
+            c.wait()
+            forward(h, d)
+    for d in (3, 5):
+        far[d].wait()
+        to_sibling(d)
+    far[4].wait()
+    far[0].wait()
+    to_sibling(4)
     for c in sib_copies:
         c.wait()
 
@@ -176,65 +218,6 @@
         return carry
 
     lax.fori_loop(0, 4, normalise, 0)
-    for c in plane:
-        c.wait()
-
-    scale = scale_ref[0]
-    ej[...] = jnp.dot(
-        ct[...].reshape(512, 768), clt[...], preferred_element_type=F32
-    ).reshape(4, 128, 512)
-    column = lax.broadcasted_iota(jnp.int32, (1, 512), 1)
-    clip_pos = (y * 2 + lax.div(column, 256)) * 1024 + x * 256 + lax.rem(column, 256)
-
-    def pass_one(b, top):
-        j = b * 128 + lax.broadcasted_iota(jnp.int32, (128, 1), 0)
-        cap_pos = ((b * 2 + zl) * 8 + lax.rem(lax.div(j, 32), 4) * 2 + core) * 128
-        cap_pos = cap_pos + zh * 32 + lax.rem(j, 32)
-        alike = vjc[b] == vir[...]
-        allowed = jnp.logical_not(alike) | (cap_pos == clip_pos)
-        s = jnp.where(allowed, scale * ej[b], NEGATIVE_FILL)
-        ej[b] = s
-        return jnp.maximum(top, jnp.max(s, axis=0, keepdims=True))
-
-    clip_top = lax.fori_loop(0, 4, pass_one, jnp.full((1, 512), NEGATIVE_FILL, F32))
-
-    def pass_two(b, total):
-        e = jnp.exp(ej[b] - clip_top)
-        ek[b] = e
-        return total + jnp.sum(e, axis=0, keepdims=True)
-
-    clip_sum = lax.fori_loop(0, 4, pass_two, jnp.zeros((1, 512), F32))
-    for b in range(4):
-        rst[b:b + 1, :] = clip_top[:, b * 128:(b + 1) * 128]
-        rst[4 + b:5 + b, :] = clip_sum[:, b * 128:(b + 1) * 128]
-    stats = []
-    for d in others_z + (0,):
-        for i in range(2):
-            if d or i:
-                n = i * 8 + d
-                device = chip(x, y, lax.rem(z + d, 8), core if i == 0 else 1 - core)
-                stats.append(copy(rst, rz.at[n], t_s.at[0, n], t_r.at[0, n], device))
-
-    def pass_three(b, carry):
-        s = ej[b]
-        top = jnp.max(s, axis=1, keepdims=True)
-        e = jnp.exp(s - top)
-        ej[b] = e
-        cst[pl.ds(b, 1), :] = to_row(top)
-        cst[pl.ds(4 + b, 1), :] = to_row(jnp.sum(e, axis=1, keepdims=True))
-        return carry
-
-    lax.fori_loop(0, 4, pass_three, 0)
-    for i, j in others_xy:
-        n = i * 4 + j
-        stats.append(copy(cst, cz.at[n], t_s.at[1, n], t_r.at[1, n], at_xy(i, j)))
-    rz[0] = rst[...]
-    cz[0] = cst[...]
-
-    def joined(ref):
-        tops = ref[:, 0:4]
-        top = jnp.max(tops, axis=0)
-        return top + jnp.log(jnp.sum(ref[:, 4:8] * jnp.exp(tops - top), axis=0))
 
     edge_copies = []
     for r in range(2):
@@ -257,6 +240,63 @@
         edge_copies.append(
             copy(eo.at[2 * r + 1], ei.at[side * 2], e_s.at[2 * r + 1], e_r.at[side * 2], device)
         )
+    for c in stage_b:
+        c.wait()
+
+    scale = scale_ref[0]
+    ej[...] = jnp.dot(
+        ct[...].reshape(512, 768), clt[...], preferred_element_type=F32
+    ).reshape(4, 128, 512)
+    column = lax.broadcasted_iota(jnp.int32, (1, 512), 1)
+    clip_pos = (y * 2 + lax.div(column, 256)) * 1024 + x * 256 + lax.rem(column, 256)
+
+    def pass_one(b, top):
+        j = b * 128 + lax.broadcasted_iota(jnp.int32, (128, 1), 0)
+        half = lax.div(j, 256)
+        first = lax.rem(lax.div(j, 64), 4)
+        second = lax.rem(lax.div(j, 16), 4)
+        ypos = jnp.where(half == 0, first, second)
+        xpos = jnp.where(half == 0, second, first)
+        cap_pos = ((ypos * 2 + zl) * 8 + xpos * 2 + core) * 128 + zh * 32 + half * 16 + lax.rem(j, 16)
+        alike = vjc[b] == vir[...]
+        allowed = jnp.logical_not(alike) | (cap_pos == clip_pos)
+        s = jnp.where(allowed, scale * ej[b], NEGATIVE_FILL)
+        ek[b] = s
+        high = jnp.max(s, axis=1, keepdims=True)
+        e = jnp.exp(s - high)
+        ej[b] = e
+        high = to_row(high)
+        ctop[pl.ds(b, 1), :] = high
+        cst[pl.ds(b, 1), :] = high + jnp.log(to_row(jnp.sum(e, axis=1, keepdims=True)))
+        return jnp.maximum(top, jnp.max(s, axis=0, keepdims=True))
+
+    clip_top = lax.fori_loop(0, 4, pass_one, jnp.full((1, 512), NEGATIVE_FILL, F32))
+    stats = []
+    for i, j in others_xy:
+        n = i * 4 + j
+        stats.append(copy(cst, cz.at[n], t_s.at[1, n], t_r.at[1, n], at_xy(i, j)))
+
+    def pass_two(b, total):
+        e = jnp.exp(ek[b] - clip_top)
+        ek[b] = e
+        return total + jnp.sum(e, axis=0, keepdims=True)
+
+    clip_lse = clip_top + jnp.log(lax.fori_loop(0, 4, pass_two, jnp.zeros((1, 512), F32)))
+    for b in range(4):
+        rst[b:b + 1, :] = clip_lse[:, b * 128:(b + 1) * 128]
+    for d in others_z + (0,):
+        for i in range(2):
+            if d or i:
+                n = i * 8 + d
+                device = chip(x, y, lax.rem(z + d, 8), core if i == 0 else 1 - core)
+                stats.append(copy(rst, rz.at[n], t_s.at[0, n], t_r.at[0, n], device))
+    rz[0] = rst[...]
+    cz[0] = cst[...]
+
+    def joined(ref):
+        values = ref[...]
+        top = jnp.max(values, axis=0)
+        return top + jnp.log(jnp.sum(jnp.exp(values - top), axis=0))
 
     for b in range(4):
         ejt[:, b * 128:(b + 1) * 128] = ej[b].T
@@ -295,12 +335,13 @@
 
     for c in stats:
         c.wait()
-    clip_fac = 0.5 * jnp.exp(rst[0:4] - joined(rz))
-    cap_fac = 0.5 * jnp.exp(cst[0:4] - joined(cz))
-    clip_line = jnp.concatenate([clip_fac[b:b + 1] for b in range(4)], axis=1)
+    whole = joined(rz)
+    whole = jnp.concatenate([whole[b:b + 1] for b in range(4)], axis=1)
+    clip_line = 0.5 * jnp.exp(clip_top - whole)
+    for b in range(4):
+        rst[b:b + 1, :] = clip_line[:, b * 128:(b + 1) * 128]
+    cap_fac = 0.5 * jnp.exp(ctop[...] - joined(cz))
     cap_line = jnp.concatenate([cap_fac[b:b + 1] for b in range(4)], axis=1)
-    rst[0:4] = clip_fac
-    cst[0:4] = cap_fac
 
     def weigh(c):
         blocks = [c, 2 + c]
@@ -319,46 +360,87 @@
     for r, part in enumerate(weigh(1 - core)):
         g[r] = part.astype(BF16).reshape(4, 32, 768)
         sib_copies.append(copy(g.at[r], sb.at[r], w_s.at[0, r], w_r.at[0, r], sibling))
-    for r, part in enumerate(weigh(core)):
-        hown[r] = part.reshape(4, 32, 768)
-
-
-    back = []
-
-    def caption_part(offsets):
-        blocks = [lax.rem(y + j, 4) for j in offsets]
+
+    stage_a = []
+
+    def caption_part(h):
         w = [
-            (ek[b] * clip_line + ej[b] * to_col(cst[pl.ds(b, 1), :])).astype(BF16) for b in blocks
+            (ek[b] * clip_line + ej[b] * to_col(cap_fac[b:b + 1])).astype(BF16)
+            for b in (2 * h, 2 * h + 1)
         ]
         part = lax.dot_general(
             jnp.concatenate(w, axis=0), clt[...], (((1,), (1,)), ((), ())),
             preferred_element_type=F32,
-        ).reshape(2, 4, 32, 768)
-        for n, j in enumerate(offsets):
-            g2[j] = part[n].astype(BF16)
-            if j == 0:
-                pc[...] = part[n]
-            for i in (2, 1, 3, 0):
-                if i or j:
-                    src = g2.at[j, lax.rem(x + i, 4)]
-                    back.append(
-                        copy(src, got.at[i * 4 + j], v_s.at[i, j], v_r.at[i, j], at_xy(i, j))
-                    )
-
-    caption_part((2, 1))
-    z_copies = []
+        ).reshape(4, 4, 16, 768)
+        pc[h] = part
+        g2[h] = part.astype(BF16)
+        at, to, first = ((at_y, qy, y), (at_x, qx, x))[h]
+        for d in (2, 1, 3):
+            src = g2.at[h, lax.rem(first + d, 4)]
+            stage_a.append(copy(src, to.at[d], v_s.at[h, d], v_r.at[h, d], at(d)))
+
+    caption_part(0)
+    caption_part(1)
+    for r, part in enumerate(weigh(core)):
+        hown[r] = part.reshape(4, 32, 768)
+
     for c in sib_copies:
         c.wait()
     for r in range(2):
         both = hown[r] + sb[r].astype(F32)
         hown[r] = both
         hb[r] = both.astype(BF16)
-    for d in others_z:
+
+    def piece(d):
         to = lax.rem(z + d, 8)
-        src = hb.at[lax.rem(to, 2), lax.div(to, 2)]
-        z_copies.append(copy(src, rzs.at[d], w_s.at[1, d], w_r.at[1, d], at_z(d)))
-    caption_part((3, 0))
-    for c in back:
+        return lax.rem(to, 2), lax.div(to, 2)
+
+    upper, lower = pl.ds(0, 16), pl.ds(16, 16)
+    first = []
+    z_copies = []
+    for n, (to, d) in enumerate(((2, 3), (6, 5))):
+        first.append(
+            copy(hb.at[piece(d)], s1.at[n], x_s.at[0, n], x_r.at[0, n], at_z(to))
+        )
+    for n, (to, rows16) in enumerate(((2, upper), (6, lower))):
+        first.append(
+            copy(hb.at[(*piece(4), rows16)], s1h.at[n], x_s.at[1, n], x_r.at[1, n], at_z(to))
+        )
+    for n, (to, rows16) in enumerate(((2, lower), (6, upper))):
+        z_copies.append(
+            copy(hb.at[(*piece(to), rows16)], r2z.at[n, rows16], x_s.at[2, n], x_r.at[2, n], at_z(to))
+        )
+    for n, d in enumerate((1, 7)):
+        first[n].wait()
+        a, b = piece(d)
+        m1[n] = (hown[a, b] + s1[n].astype(F32)).astype(BF16)
+        z_copies.append(copy(m1.at[n], r1z.at[n], x_s.at[3, n], x_r.at[3, n], at_z(d)))
+    for n, (d, rows16) in enumerate(((2, upper), (6, lower))):
+        first[2 + n].wait()
+        a, b = piece(d)
+        m2[n] = (hown[a, b, rows16] + s1h[n].astype(F32)).astype(BF16)
+        z_copies.append(
+            copy(m2.at[n], r2z.at[n, rows16], x_s.at[4, n], x_r.at[4, n], at_z(d))
+        )
+
+    stage_b = []
+    for c in stage_a[:3]:
+        c.wait()
+    total = pc[0, y] + qy[1].astype(F32) + qy[2].astype(F32) + qy[3].astype(F32)
+    r0[...] = total
+    r0b[...] = total.astype(BF16)
+    for d in (2, 1, 3):
+        src = r0b.at[lax.rem(x + d, 4)]
+        stage_b.append(copy(src, fx.at[d], v_s.at[2, d], v_r.at[2, d], at_x(d)))
+    for c in stage_a[3:]:
+        c.wait()
+    total = pc[1, x] + qx[1].astype(F32) + qx[2].astype(F32) + qx[3].astype(F32)
+    r1[...] = total
+    r1b[...] = total.astype(BF16)
+    for d in (2, 1, 3):
+        src = r1b.at[lax.rem(y + d, 4)]
+        stage_b.append(copy(src, fy.at[d], v_s.at[3, d], v_r.at[3, d], at_y(d)))
+    for c in stage_b:
         c.wait()
 
     def ordered(v):
@@ -366,9 +448,9 @@
         tails = [v[:, 512 + 64 * i:576 + 64 * i] for i in range(4)]
         return jnp.concatenate([t for pair in zip(tiles, tails) for t in pair], axis=1)
 
-    acc = pc[x]
-    for n in range(1, 16):
-        acc = acc + got[n].astype(F32)
+    low = r0[x] + fx[1].astype(F32) + fx[2].astype(F32) + fx[3].astype(F32)
+    high = r1[y] + fy[1].astype(F32) + fy[2].astype(F32) + fy[3].astype(F32)
+    acc = jnp.concatenate([low, high], axis=0)
     held = hcap[...]
     clip_held = hclip[...]
     clip_unit = clip_held.astype(BF16).astype(F32)
@@ -381,9 +463,8 @@
 
     for c in z_copies:
         c.wait()
-    acc = hown[zl, zh]
-    for d in range(1, 8):
-        acc = acc + rzs[d].astype(F32)
+    acc = hown[zl, zh] + r1z[0].astype(F32) + r1z[1].astype(F32)
+    acc = acc + r2z[0].astype(F32) + r2z[1].astype(F32)
     grad = scale * acc - 0.5 * scale * cap_unit
     dclip_ref[...] = ordered(
         (grad - clip_held * jnp.sum(clip_held * grad, axis=1, keepdims=True)) / hlen[0]
@@ -406,17 +487,25 @@
             V((2, 192, 128), BF16), V((64, 128), jnp.int32),
             V((4, 48, 128), BF16), V((4, 48, 128), BF16), V((16, 192, 128), BF16),
             V((32, 768), F32), V((32, 768), F32), V((2, 32, 1), F32),
-            V((768, 512), BF16), V((16, 32, 768), BF16),
+            V((768, 512), BF16), V((2, 4, 4, 16, 768), BF16),
             V((4, 128, 1), F32), V((1, 512), F32), V((1, 512), F32), V((4, 128, 1), F32),
             V((4, 128, 768), F32), V((4, 128, 1), F32), V((4, 1, 768), F32), V((4, 1, 768), F32),
             V((4, 128, 512), F32), V((4, 128, 512), F32), V((512, 512), F32), V((512, 512), F32),
-            V((4, 128, 768), F32),
-            V((8, 128), F32), V((16, 8, 128), F32), V((8, 128), F32), V((16, 8, 128), F32),
+            V((4, 128, 768), F32), V((4, 128), F32),
+            V((4, 128), F32), V((16, 4, 128), F32), V((4, 128), F32), V((16, 4, 128), F32),
             V((2, 4, 32, 768), BF16), V((2, 4, 32, 768), BF16), V((2, 4, 32, 768), BF16),
-            V((2, 4, 32, 768), F32), V((8, 32, 768), BF16),
-            V((4, 32, 768), F32), V((4, 4, 32, 768), BF16), V((16, 32, 768), BF16),
-            dma(3), dma(4), dma(4), dma(8), dma(8), dma(8), dma(8), dma(4, 4), dma(4, 4),
-            dma(4), dma(4), dma(2, 16), dma(2, 16), dma(2, 8), dma(2, 8), dma(4, 4), dma(4, 4),
+            V((2, 4, 32, 768), F32), V((2, 32, 768), BF16), V((2, 16, 768), BF16),
+            V((2, 32, 768), BF16), V((2, 16, 768), BF16), V((2, 32, 768), BF16),
+            V((2, 32, 768), BF16),
+            V((2, 4, 4, 16, 768), BF16), V((2, 4, 4, 16, 768), F32),
+            V((4, 4, 16, 768), BF16), V((4, 4, 16, 768), BF16),
+            V((4, 16, 768), F32), V((4, 16, 768), F32),
+            V((4, 16, 768), BF16), V((4, 16, 768), BF16),
+            V((4, 16, 768), BF16), V((4, 16, 768), BF16),
+            dma(3), dma(4), dma(4), dma(8), dma(8), dma(8), dma(8), dma(2, 4), dma(2, 4),
+            dma(2, 4, 4), dma(2, 4, 4),
+            dma(4), dma(4), dma(2, 16), dma(2, 16), dma(1, 2), dma(1, 2), dma(5, 2), dma(5, 2),
+            dma(4, 4), dma(4, 4),
         ],
         compiler_params=pltpu.CompilerParams(
             collective_id=0, has_side_effects=True, vmem_limit_bytes=48 * 1024 * 1024

time: 53.8 us -> 48.9 us (0.909)
  Pallas kernels: 51 us -> 46.2 us
    pallas_call x1, Pallas kernels: 51 us -> 46.2 us  [body(): pl.pallas_call(kernel, out_shape=(out, out), in_specs=[pl.BlockSpec(memor...]
where the time goes in v3:
time: 48.9 us; the launch traced here: 48.8 us
  Pallas kernels  46.2 us (94%)
  between operations  1.29 us (3%)
  local copies, waits for them, and re-layouts  1.28 us (3%)
    pallas_call x1, Pallas kernels, body(): pl.pallas_call(kernel, out_shape=(out, out), in_specs=[pl.BlockSpec(memor...  46.2 us
    unnamed x2, local copies, waits for them, and re-layouts  1.28 us

profile of v3, /device:TPU:1, one launch (start us, length us, event | category | flops | bytes accessed | tf_op | source)
XLA Modules:
  0.0 48.8 jit_solution(15606455882999944862)
XLA Ops:
  1.3 46.2 %contrastive.1 = (f32[32,768]{1,0:T(8,128)S(1)}, f32[32,768]{1,0:T(8,128)S(1)}) custom-call(f32[1]{0:T(128)} %bitcast.4.scale_ref, s32[64,128]{1,0:T(8,128)} %bitcast.7, bf16[192,128]{1,0:T(8,128)(2,1)} %bitcast.5, bf16[192,128]{1,0:T(8,128)(2,1)} %bitcast.6), custom_call_target="tpu_custom_call" | custom-call | tf_op jit(solution)/shard_map/contrastive/pallas_call | solution.py:481
  47.5 0.6 %copy.9 = f32[32,768]{1,0:T(8,128)} copy(f32[32,768]{1,0:T(8,128)S(1)} %get-tuple-element.4) | data formatting | bytes 196608
  48.1 0.6 %copy.10 = f32[32,768]{1,0:T(8,128)} copy(f32[32,768]{1,0:T(8,128)S(1)} %get-tuple-element.5) | data formatting | bytes 196608

commit v4 on v3

--- a/solution.py
+++ b/solution.py
@@ -147,8 +147,6 @@
         far[sem] = copy(ref, ref, z_s.at[sem], z_r.at[sem], at_z(to))
         to_sibling(d)
 
-    relay(1, 2, 3, None)
-    relay(7, 6, 5, None)
 
     def unpacked(parts):
         low = lax.broadcasted_iota(jnp.int32, (16, 128), 1) < 64
@@ -188,10 +186,12 @@
         for d in (2, 1, 3):
             stage_b.append(copy(ref, ref, f_s.at[h, e, d], f_r.at[h, e, d], across(d)))
 
+    relay(1, 2, 3, None)
+    relay(7, 6, 5, None)
+    relay(2, 2, 4, 0)
+    relay(6, 6, 0, 96)
     forward(0, 0)
     forward(1, 0)
-    relay(2, 2, 4, 0)
-    relay(6, 6, 0, 96)
     for n in (1, 2, 0):
         for h in range(2):
             d, c = stage_a[h][n]
@@ -456,7 +456,7 @@
     clip_unit = clip_held.astype(BF16).astype(F32)
     cap_unit = held.astype(BF16).astype(F32)
     pool_unit = pu[home, rows, :]
-    grad = scale * acc - 0.5 * scale * clip_unit - 0.5 * scale * pool_unit
+    grad = acc - 0.5 * clip_unit - 0.5 * pool_unit
     dcap_ref[...] = ordered(
         (grad - held * jnp.sum(held * grad, axis=1, keepdims=True)) / hlen[1]
     )
@@ -465,7 +465,7 @@
         c.wait()
     acc = hown[zl, zh] + r1z[0].astype(F32) + r1z[1].astype(F32)
     acc = acc + r2z[0].astype(F32) + r2z[1].astype(F32)
-    grad = scale * acc - 0.5 * scale * cap_unit
+    grad = acc - 0.5 * cap_unit
     dclip_ref[...] = ordered(
         (grad - clip_held * jnp.sum(clip_held * grad, axis=1, keepdims=True)) / hlen[0]
     )
@@ -478,7 +478,7 @@
     out = jax.ShapeDtypeStruct((32, 768), F32)
     V = pltpu.VMEM
     keep = lambda v: pltpu.with_memory_space_constraint(v, pltpu.HBM)
-    return pl.pallas_call(
+    d_clips, d_captions = pl.pallas_call(
         kernel,
         out_shape=(out, out),
         in_specs=[pl.BlockSpec(memory_space=pltpu.SMEM), hbm, hbm, hbm],
@@ -512,6 +512,7 @@
         ),
         name="contrastive",
     )(logit_scale.reshape(1), keep(video_id.reshape(64, 128)), keep(clips.T), keep(captions.T))
+    return logit_scale * d_clips, logit_scale * d_captions
 
 
 def solution(mesh):

time: 48.9 us -> 47.2 us (0.965)
  local copies, waits for them, and re-layouts: 1.28 us -> 0 us
  Pallas kernels: 46.2 us -> 45.1 us
  other arithmetic: 0 us -> 0.69 us
    unnamed x2 -> x0, local copies, waits for them, and re-layouts: 1.28 us -> none
    pallas_call x1, Pallas kernels: 46.2 us -> 45.1 us  [body(): pl.pallas_call(kernel, out_shape=(out, out), in_specs=[pl.BlockSpec(memor...]
    mul x0 -> x1, other arithmetic: none -> 0.69 us  [body(): return (logit_scale * d_clips, logit_scale * d_captions)]
where the time goes in v4:
time: 47.2 us; the launch traced here: 47.1 us
  Pallas kernels  45.1 us (96%)
  between operations  1.29 us (3%)
  other arithmetic  0.69 us (1%)
    pallas_call x1, Pallas kernels, body(): pl.pallas_call(kernel, out_shape=(out, out), in_specs=[pl.BlockSpec(memor...  45.1 us

profile of v4, /device:TPU:1, one launch (start us, length us, event | category | flops | bytes accessed | tf_op | source)
XLA Modules:
  0.0 47.1 jit_solution(362580168584324989)
XLA Ops:
  1.3 45.1 %contrastive.1 = (f32[32,768]{1,0:T(8,128)S(1)}, f32[32,768]{1,0:T(8,128)S(1)}) custom-call(f32[1]{0:T(128)} %bitcast.4.scale_ref, s32[64,128]{1,0:T(8,128)} %bitcast.7, bf16[192,128]{1,0:T(8,128)(2,1)} %bitcast.5, bf16[192,128]{1,0:T(8,128)(2,1)} %bitcast.6), custom_call_target="tpu_custom_call" | custom-call | tf_op jit(solution)/shard_map/contrastive/pallas_call | solution.py:481
  46.4 0.7 %broadcast_multiply_fusion = (f32[32,768]{1,0:T(8,128)}, f32[32,768]{1,0:T(8,128)}) fusion(f32[32,768]{1,0:T(8,128)S(1)} %get-tuple-element.5, f32[]{:T(128)} %copy.6, f32[32,768]{1,0:T(8,128)S(1)} %get-tuple-element.4), kind=kLoop, calls=%fused_computation | loop fusion | flops 49152 | bytes 393220 | tf_op jit(solution)/shard_map/mul | solution.py:515

commit v5 on v4

--- a/solution.py
+++ b/solution.py
@@ -363,15 +363,16 @@
 
     stage_a = []
 
+    w = [
+        (ek[b] * clip_line + ej[b] * to_col(cap_fac[b:b + 1])).astype(BF16) for b in range(4)
+    ]
+    both_halves = lax.dot_general(
+        jnp.concatenate(w, axis=0), clt[...], (((1,), (1,)), ((), ())),
+        preferred_element_type=F32,
+    ).reshape(2, 4, 4, 16, 768)
+
     def caption_part(h):
-        w = [
-            (ek[b] * clip_line + ej[b] * to_col(cap_fac[b:b + 1])).astype(BF16)
-            for b in (2 * h, 2 * h + 1)
-        ]
-        part = lax.dot_general(
-            jnp.concatenate(w, axis=0), clt[...], (((1,), (1,)), ((), ())),
-            preferred_element_type=F32,
-        ).reshape(4, 4, 16, 768)
+        part = both_halves[h]
         pc[h] = part
         g2[h] = part.astype(BF16)
         at, to, first = ((at_y, qy, y), (at_x, qx, x))[h]

time: 47.2 us -> 47.2 us (level)
  no operation moved by 1% of the time
where the time goes in v5:
time: 47.2 us; the launch traced here: 47.1 us
  Pallas kernels  45.1 us (96%)
  between operations  1.29 us (3%)
  other arithmetic  0.69 us (1%)
    pallas_call x1, Pallas kernels, body(): pl.pallas_call(kernel, out_shape=(out, out), in_specs=[pl.BlockSpec(memor...  45.1 us

profile of v5, /device:TPU:1, one launch (start us, length us, event | category | flops | bytes accessed | tf_op | source)
XLA Modules:
  0.0 47.1 jit_solution(8385140455514449909)
XLA Ops:
  1.3 45.1 %contrastive.1 = (f32[32,768]{1,0:T(8,128)S(1)}, f32[32,768]{1,0:T(8,128)S(1)}) custom-call(f32[1]{0:T(128)} %bitcast.4.scale_ref, s32[64,128]{1,0:T(8,128)} %bitcast.7, bf16[192,128]{1,0:T(8,128)(2,1)} %bitcast.5, bf16[192,128]{1,0:T(8,128)(2,1)} %bitcast.6), custom_call_target="tpu_custom_call" | custom-call | tf_op jit(solution)/shard_map/contrastive/pallas_call | solution.py:482
  46.4 0.7 %broadcast_multiply_fusion = (f32[32,768]{1,0:T(8,128)}, f32[32,768]{1,0:T(8,128)}) fusion(f32[32,768]{1,0:T(8,128)S(1)} %get-tuple-element.5, f32[]{:T(128)} %copy.6, f32[32,768]{1,0:T(8,128)S(1)} %get-tuple-element.4), kind=kLoop, calls=%fused_computation | loop fusion | flops 49152 | bytes 393220 | tf_op jit(solution)/shard_map/mul | solution.py:516

commit v6 on v5

--- a/solution.py
+++ b/solution.py
@@ -25,7 +25,7 @@
     ej, ek, ejt, ekt, pj, ctop,
     rst, rz, cst, cz,
     g, sb, hb, hown, s1, s1h, m1, m2, r1z, r2z,
-    g2, pc, qy, qx, r0, r1, r0b, r1b, fx, fy,
+    g2, qy, qx, r0, r1, r0b, r1b, fx, fy,
     l_s, a2a_s, a2a_r, z_s, z_r, s_s, s_r, p_s, p_r, f_s, f_r, e_s, e_r,
     t_s, t_r, w_s, w_r, x_s, x_r, v_s, v_r,
 ):
@@ -373,7 +373,6 @@
 
     def caption_part(h):
         part = both_halves[h]
-        pc[h] = part
         g2[h] = part.astype(BF16)
         at, to, first = ((at_y, qy, y), (at_x, qx, x))[h]
         for d in (2, 1, 3):
@@ -427,7 +426,7 @@
     stage_b = []
     for c in stage_a[:3]:
         c.wait()
-    total = pc[0, y] + qy[1].astype(F32) + qy[2].astype(F32) + qy[3].astype(F32)
+    total = g2[0, y].astype(F32) + qy[1].astype(F32) + qy[2].astype(F32) + qy[3].astype(F32)
     r0[...] = total
     r0b[...] = total.astype(BF16)
     for d in (2, 1, 3):
@@ -435,7 +434,7 @@
         stage_b.append(copy(src, fx.at[d], v_s.at[2, d], v_r.at[2, d], at_x(d)))
     for c in stage_a[3:]:
         c.wait()
-    total = pc[1, x] + qx[1].astype(F32) + qx[2].astype(F32) + qx[3].astype(F32)
+    total = g2[1, x].astype(F32) + qx[1].astype(F32) + qx[2].astype(F32) + qx[3].astype(F32)
     r1[...] = total
     r1b[...] = total.astype(BF16)
     for d in (2, 1, 3):
@@ -498,7 +497,7 @@
             V((2, 4, 32, 768), F32), V((2, 32, 768), BF16), V((2, 16, 768), BF16),
             V((2, 32, 768), BF16), V((2, 16, 768), BF16), V((2, 32, 768), BF16),
             V((2, 32, 768), BF16),
-            V((2, 4, 4, 16, 768), BF16), V((2, 4, 4, 16, 768), F32),
+            V((2, 4, 4, 16, 768), BF16),
             V((4, 4, 16, 768), BF16), V((4, 4, 16, 768), BF16),
             V((4, 16, 768), F32), V((4, 16, 768), F32),
             V((4, 16, 768), BF16), V((4, 16, 768), BF16),

time: 47.2 us -> 47.3 us (level)
  no operation moved by 1% of the time
where the time goes in v6:
time: 47.3 us; the launch traced here: 47.1 us
  Pallas kernels  45.1 us (95%)
  between operations  1.29 us (3%)
  other arithmetic  0.69 us (1%)
    pallas_call x1, Pallas kernels, body(): pl.pallas_call(kernel, out_shape=(out, out), in_specs=[pl.BlockSpec(memor...  45.1 us

profile of v6, /device:TPU:1, one launch (start us, length us, event | category | flops | bytes accessed | tf_op | source)
XLA Modules:
  0.0 47.1 jit_solution(10608585709631044472)
XLA Ops:
  1.3 45.1 %contrastive.1 = (f32[32,768]{1,0:T(8,128)S(1)}, f32[32,768]{1,0:T(8,128)S(1)}) custom-call(f32[1]{0:T(128)} %bitcast.4.scale_ref, s32[64,128]{1,0:T(8,128)} %bitcast.7, bf16[192,128]{1,0:T(8,128)(2,1)} %bitcast.5, bf16[192,128]{1,0:T(8,128)(2,1)} %bitcast.6), custom_call_target="tpu_custom_call" | custom-call | tf_op jit(solution)/shard_map/contrastive/pallas_call | solution.py:481
  46.4 0.7 %broadcast_multiply_fusion = (f32[32,768]{1,0:T(8,128)}, f32[32,768]{1,0:T(8,128)}) fusion(f32[32,768]{1,0:T(8,128)S(1)} %get-tuple-element.5, f32[]{:T(128)} %copy.6, f32[32,768]{1,0:T(8,128)S(1)} %get-tuple-element.4), kind=kLoop, calls=%fused_computation | loop fusion | flops 49152 | bytes 393220 | tf_op jit(solution)/shard_map/mul | solution.py:515
